TPU v7x, 32 devices: a whole 2x2x4 slice. The times are simulated.
32 devices in a mesh: row: 4 (over y, x), col: 8 (over z, core).
Axes of the slice: x: 2, y: 2, z: 4, core: 2. Of those that a mesh axis runs over, the one named last changes fastest.
Arguments:
- slab: bfloat16 [1024, 16384], P(('row', 'col')), may hold values from -0.1875 to 0.1875
- block_mask: int32 [32, 16], P(('row', 'col')), may hold values 0 or 1
- damping: float32 [16384], replicated, may hold values from 0.05 to 2
Outputs:
- hessian: float32 [16384, 16384], P('row', 'col')
All inputs are finite; a program needn't handle non-finite values. No bound on the sum of `block_mask` on one device may be relied on, other than what follows from the above.
Results may differ from a plain program's by a relative error of at most 0.0003.
Values may be sent and summed in bfloat16 or wider, within the bound.
No kernel may reach another device: no remote copies, remote signals or barrier semaphores. Data moves between devices by JAX's collectives and lax.ppermute only.
A program may use at most 128 MiB of HBM per device.

v0:
```python
import jax
import jax.numpy as jnp
from jax import lax
from jax.sharding import PartitionSpec as P


def shards(slab, block_mask, damping):
    local_rows = slab.shape[0]
    width = slab.shape[1]
    row_count = lax.axis_size("row")
    col_count = lax.axis_size("col")
    row_width = width // row_count
    col_width = width // col_count
    block_count = block_mask.shape[1]
    column_mask = jnp.repeat(block_mask[0], width // block_count).astype(jnp.bfloat16)
    masked = slab * column_mask[None, :]
    row_parts = masked.reshape(local_rows, row_count, row_width)
    row_parts = lax.all_to_all(row_parts, "row", split_axis=1, concat_axis=0, tiled=True)
    row_parts = row_parts.reshape(row_count * local_rows, row_width)
    row_panel = lax.all_gather(row_parts, "col", axis=0, tiled=True)
    row_panel = row_panel.reshape(col_count, row_count, local_rows, row_width)
    row_panel = jnp.transpose(row_panel, (1, 0, 2, 3)).reshape(
        row_count * col_count * local_rows, row_width
    )
    col_parts = masked.reshape(local_rows, col_count, col_width)
    col_parts = lax.all_to_all(col_parts, "col", split_axis=1, concat_axis=0, tiled=True)
    col_parts = col_parts.reshape(col_count * local_rows, col_width)
    block = lax.dot_general(
        row_panel,
        lax.all_gather(col_parts, "row", axis=0, tiled=True),
        (((0,), (0,)), ((), ())),
        preferred_element_type=jnp.float32,
    )
    row_start = lax.axis_index("row") * row_width
    col_start = lax.axis_index("col") * col_width
    global_rows = row_start + jnp.arange(row_width, dtype=jnp.int32)
    global_cols = col_start + jnp.arange(col_width, dtype=jnp.int32)
    row_damping = lax.dynamic_slice_in_dim(damping, row_start, row_width, 0)
    on_diagonal = global_rows[:, None] == global_cols[None, :]
    return block + jnp.where(on_diagonal, row_damping[:, None], jnp.float32(0.0))


def solution(mesh):
    placed = (P(("row", "col"), None), P(("row", "col"), None), P())
    return jax.shard_map(
        shards, mesh=mesh, in_specs=placed, out_specs=P("row", "col"), check_vma=False
    )
```

profile of v0, /device:TPU:1, one launch (start us, length us, event | category | flops | bytes accessed | tf_op | source)
XLA Modules:
  0.0 213.6 jit_solution(16617587774653621209)
XLA Ops:
  6.5 0.0 all-gather.3.cloned.1.call-start
  6.5 0.7 convert_bitcast_fusion
  7.2 0.1 broadcast_bitcast_fusion
  7.3 1.4 broadcast_multiply_fusion
  8.6 0.1 copy.17
  8.7 17.0 %all_to_all.30 = bf16[32,4,4096]{2,0,1:T(8,128)(2,1)} all-to-all(bf16[32,4,4096]{2,0,1:T(8,128)(2,1)S(1)} %bitcast.36), channel_id=1, replica_groups=mesh['row'=4,'col'=8] {'row'}, dimensions={1} | all-to-all | bytes 2097152 | tf_op jit(solution)/shard_map/all_to_all | solution.py:18
  25.8 0.0 all-gather.3.cloned.1.call-update
  25.8 0.0 all-gather.5.cloned.1.call-start
  25.9 0.1 copy.16
  26.0 55.5 %all_to_all.31 = bf16[32,8,2048]{2,0,1:T(8,128)(2,1)} all-to-all(bf16[32,8,2048]{2,0,1:T(8,128)(2,1)S(1)} %bitcast.35), channel_id=1, replica_groups=mesh['row'=4,'col'=8] {'col'}, dimensions={1} | all-to-all | bytes 2097152 | tf_op jit(solution)/shard_map/all_to_all | solution.py:26
  81.4 0.0 all-gather.5.cloned.1.call-update
  81.5 47.0 %all-gather.3.cloned.1.call-done = bf16[1024,4096]{1,0:T(8,128)(2,1)} async-done(((bf16[128,4096]{1,0:T(8,128)(2,1)}), bf16[1024,4096]{1,0:T(8,128)(2,1)}) %all-gather.3.cloned.1.call-update) | async-done | bytes 8388624 | tf_op jit(solution)/shard_map/all_gather | solution.py:20
  128.4 0.0 dynamic-slice-start
  128.4 8.2 %copy.9 = bf16[8,4,32,4096]{3,2,0,1:T(8,128)(2,1)} copy(bf16[8,4,32,4096]{3,2,1,0:T(8,128)(2,1)} %bitcast.31) | data formatting | bytes 16777216 | tf_op jit(solution)/shard_map/reshape | solution.py:21
  136.6 43.4 %all-gather.5.cloned.1.call-done = bf16[1024,2048]{1,0:T(8,128)(2,1)} async-done(((bf16[256,2048]{1,0:T(8,128)(2,1)}), bf16[1024,2048]{1,0:T(8,128)(2,1)}) %all-gather.5.cloned.1.call-update) | async-done | bytes 4194320 | tf_op jit(solution)/shard_map/all_gather | solution.py:30
  180.0 0.0 dynamic-slice-done
  180.0 26.7 %select_add_fusion = f32[4096,2048]{1,0:T(8,128)} fusion(bf16[1024,4096]{1,0:T(8,128)(2,1)} %bitcast.32, bf16[1024,2048]{1,0:T(8,128)(2,1)} %all-gather.5.cloned.1.call-done, f32[4096]{0:T(1024)S(1)} %dynamic-slice-done, s32[2048]{0:T(1024)S(1)} %iota_add_fusion.1, s32[4096]{0:T(1024)S(1)} %iota_add_fusion), kind=kOutput, calls=%fused_computation | convolution fusion | flops 17205035008 | bytes 46178304 | tf_op jit(solution)/shard_map/dot_general | solution.py:28
  (3 shorter events, 0.0 us)
Async XLA Ops:
  6.5 121.9 %all-gather.3.cloned.1.call-start = ((), (), s32[]{:S(2)}) async-start(), calls=%async_computation.2 | async-start | bytes 9437184 | tf_op jit(solution)/shard_map/all_gather | solution.py:20
  25.8 154.2 %all-gather.5.cloned.1.call-start = ((), (), s32[]{:S(2)}) async-start(), calls=%async_computation.3 | async-start | bytes 5242880 | tf_op jit(solution)/shard_map/all_gather | solution.py:30
  128.4 51.6 %dynamic-slice-start = ((f32[16384]{0:T(1024)}, s32[]{:T(128)}), f32[4096]{0:T(1024)S(1)}, s32[]{:S(2)}) async-start(f32[16384]{0:T(1024)} %param.5, s32[]{:T(128)} %select_n.7), calls=%async_computation.4 | async-start | bytes 33280 | tf_op jit(solution)/shard_map/dynamic_slice | solution.py:38
Sparse Core Ops, SparseCore 0:
  25.9 102.4 all-gather.2
  130.3 49.7 all-gather.4
where the time goes:
time: 214 us
  waiting for transfers between devices  90.4 us (42%)
  blocking collectives  72.5 us (34%)
  matrix products  26.7 us (12%)
  between operations  13.4 us (6%)
  local copies, waits for them, and re-layouts  8.43 us (4%)
    all_to_all x1, blocking collectives, shards(): lax.all_to_all(col_parts, 'col', split_axis=1, concat_axis=0, tiled=True)  55.5 us
    all_gather x1, waiting for transfers between devices, shards(): row_panel = lax.all_gather(row_parts, 'col', axis=0, tiled=True)  47 us
    all_gather x1, waiting for transfers between devices, shards(): lax.all_gather(col_parts, 'row', axis=0, tiled=True)  43.4 us
    dot_general x1, matrix products, shards(): lax.dot_general(row_panel, lax.all_gather(col_parts, 'row', axis=0, tiled...  26.7 us
    all_to_all x1, blocking collectives, shards(): lax.all_to_all(row_parts, 'row', split_axis=1, concat_axis=0, tiled=True)  17 us
    reshape x1, local copies, waits for them, and re-layouts, shards(): row_panel = row_panel.reshape(col_count, row_count, local_rows, row_width)  8.15 us
  transfers between devices with their start and end apart: 2, of which 2 were waited for; matrix products, arithmetic and copies ran while one was open for 4% of the time, Pallas kernels for 0%

commit v1 on v0

v1 whole, which is shorter than its diff:
```python
import functools
import math

import jax
import jax.numpy as jnp
from jax import lax
from jax.experimental import pallas as pl
from jax.experimental.pallas import tpu as pltpu
from jax.sharding import PartitionSpec as P

AXES = ("row", "col")
CORES = 2
CHUNKS = (20, 12)
BLOCK_ROWS = 512


def pick_kernel(place, mask, slab, *outs):
    blocks = mask.shape[0]
    span = slab.shape[1] // blocks
    for slot, out in enumerate(outs):
        width = out.shape[1]
        step = min(width, span)
        for part in range(width // step):
            start = place[slot] * width + part * step
            start = pl.multiple_of(start, step)
            keep = mask[start // span].astype(jnp.float32)
            piece = slab[:, pl.ds(start, step)].astype(jnp.float32)
            out[:, part * step : (part + 1) * step] = (piece * keep).astype(out.dtype)


def pick_panels(slab, mask, place, width):
    count = place.shape[0]
    rows = slab.shape[0]
    return pl.pallas_call(
        pick_kernel,
        out_shape=[jax.ShapeDtypeStruct((rows, width), slab.dtype)] * count,
        in_specs=[
            pl.BlockSpec(memory_space=pltpu.SMEM),
            pl.BlockSpec(memory_space=pltpu.SMEM),
            pl.BlockSpec(memory_space=pltpu.VMEM),
        ],
        out_specs=[pl.BlockSpec(memory_space=pltpu.VMEM)] * count,
        name="pick_panels",
    )(place, mask, slab)


def product_kernel(count, first, aliased, where, col, damp, *refs):
    parts = refs[:count]
    out = refs[-1]
    step = pl.program_id(0)
    rows, cols = out.shape
    left = jnp.concatenate([part[...] for part in parts], axis=0)
    out[...] = lax.dot_general(
        left, col[...], (((0,), (0,)), ((), ())), preferred_element_type=jnp.float32
    )
    row_at = where[0] + first + step * rows
    col_at = where[1]

    @pl.when((row_at < col_at + cols) & (col_at < row_at + rows))
    def _():
        row_ids = lax.broadcasted_iota(jnp.int32, (rows, cols), 0) + row_at
        col_ids = lax.broadcasted_iota(jnp.int32, (rows, cols), 1) + col_at
        out[...] += jnp.where(row_ids == col_ids, damp[...], 0.0)


def product(parts, col, damp, where, total, first, block):
    depth, width = parts[0].shape
    rows = math.gcd(BLOCK_ROWS, width, first)
    steps = width // rows
    held, cols = col.shape
    count = len(parts)
    grid_spec = pltpu.PrefetchScalarGridSpec(
        num_scalar_prefetch=1,
        grid=(steps,),
        in_specs=[
            pl.BlockSpec((held, cols), lambda i, w: (0, 0)),
            pl.BlockSpec((1, cols), lambda i, w: (0, 0)),
        ]
        + [pl.BlockSpec((depth, rows), lambda i, w: (0, i))] * count
        + ([] if block is None else [pl.BlockSpec(memory_space=pl.ANY)]),
        out_specs=pl.BlockSpec((rows, cols), lambda i, w: (first // rows + i, 0)),
    )
    return pl.pallas_call(
        functools.partial(product_kernel, count, first, block is not None),
        out_shape=jax.ShapeDtypeStruct((total, cols), jnp.float32),
        grid_spec=grid_spec,
        input_output_aliases={} if block is None else {3 + count: 0},
        compiler_params=pltpu.CompilerParams(vmem_limit_bytes=40 << 20),
        cost_estimate=pl.CostEstimate(
            flops=2 * held * width * cols,
            bytes_accessed=2 * held * (width + cols) + 4 * width * cols,
            transcendentals=0,
        ),
        name="product",
    )(where, col, damp, *parts, *([] if block is None else [block]))


def shards(slab, block_mask, damping):
    lines = lax.axis_size("row")
    cols = lax.axis_size("col")
    planes = cols // CORES
    group, width = slab.shape
    panel = width // lines
    half = width // cols
    line = lax.axis_index("row")
    place = lax.axis_index("col")
    plane = place // CORES
    core = place % CORES

    def send(value, pairs):
        flat = []
        for (r0, q0, c0), (r1, q1, c1) in pairs:
            flat.append(((r0 * planes + q0) * CORES + c0, (r1 * planes + q1) * CORES + c1))
        return lax.ppermute(value, AXES, flat)

    everyone = [(r, q, c) for r in range(lines) for q in range(planes) for c in range(CORES)]

    def across_lines(value, m):
        return send(value, [((r, q, c), (r ^ m, q, c)) for r, q, c in everyone])

    def across_planes(value, k):
        return send(value, [((r, q, c), (r, q ^ k, c)) for r, q, c in everyone])

    def across_cores(value):
        return send(value, [((r, q, c), (r, q, 1 - c)) for r, q, c in everyone])

    order = [line ^ m for m in range(lines)] + [plane ^ k for k in range(planes)]
    picked = pick_panels(slab, block_mask[0], jnp.stack(order).astype(jnp.int32), panel)
    by_line, by_plane = picked[:lines], picked[lines:]

    row_parts = [by_line[0]] + [across_lines(by_line[m], m) for m in range(1, lines)]
    col_parts = [by_plane[0]] + [across_planes(by_plane[k], k) for k in range(1, planes)]

    mine = jnp.concatenate(col_parts, axis=0)
    col_lines = [mine] + [across_lines(mine, m) for m in range(1, lines)]
    stacked = jnp.stack(col_lines).reshape(lines, planes, group, panel)
    stacked = jnp.transpose(stacked, (1, 0, 2, 3)).reshape(lines * planes * group, panel)
    keep = lax.dynamic_slice_in_dim(stacked, core * half, half, 1)
    give = lax.dynamic_slice_in_dim(stacked, (1 - core) * half, half, 1)
    col_panel = jnp.concatenate([keep, across_cores(give)], axis=0)

    where = jnp.stack([line * panel, place * half]).astype(jnp.int32)
    damp = lax.dynamic_slice_in_dim(damping, place * half, half, 0)[None, :]

    share = panel // sum(CHUNKS)
    out = None
    first = 0
    for chunk in CHUNKS:
        size = chunk * share
        own = jnp.concatenate([p[:, first : first + size] for p in row_parts], axis=0)
        parts = [own]
        if planes == 4:
            near = across_planes(own, 1)
            far = across_planes(own, 2)
            mid = send(own, [((r, q, c), (r, q ^ 3, c)) for r, q, c in everyone if q in (1, 2)])
            pairs = [((r, q, c), (r, q ^ 1, c)) for r, q, c in everyone if q in (1, 2)]
            last = send(far, pairs)
            parts += [near, far, jnp.where((plane == 1) | (plane == 2), mid, last)]
        else:
            parts += [across_planes(own, k) for k in range(1, planes)]
        parts += [across_cores(p) for p in parts]
        out = product(parts, col_panel, damp, where, panel, first, out)
        first += size
    return out


def solution(mesh):
    placed = (P(("row", "col"), None), P(("row", "col"), None), P())
    return jax.shard_map(
        shards, mesh=mesh, in_specs=placed, out_specs=P("row", "col"), check_vma=False
    )
```

time: 214 us -> 225 us (1.051)
  blocking collectives: 72.5 us -> 0 us
  waiting for transfers between devices: 90.4 us -> 140 us
  starting transfers between devices: 0.04 us -> 37.4 us
  Pallas kernels: 0 us -> 29.8 us
  matrix products: 26.7 us -> 0 us
  between operations: 13.4 us -> 0.2 us
  local copies, waits for them, and re-layouts: 8.43 us -> 12.4 us
    ppermute x0 -> x26, waiting for transfers between devices: none -> 140 us  [send(): return lax.ppermute(value, AXES, flat)]
    all_gather x2 -> x0, waiting for transfers between devices: 90.4 us -> none  [the longest x1 47 us: shards(): row_panel = lax.all_gather(row_parts, 'col', axis=0, tiled=True)]
    all_to_all x2 -> x0, blocking collectives: 72.5 us -> none  [the longest x1 55.5 us: shards(): lax.all_to_all(col_parts, 'col', split_axis=1, concat_axis=0, tiled=True)]
    ppermute x0 -> x26, starting transfers between devices: none -> 37.4 us  [send(): return lax.ppermute(value, AXES, flat)]
    pallas_call x0 -> x3, Pallas kernels: none -> 29.8 us  [the longest x2 26.9 us: product(): pl.pallas_call(functools.partial(product_kernel, count, first, block is n...]
    dot_general x1 -> x0, matrix products: 26.7 us -> none  [shards(): lax.dot_general(row_panel, lax.all_gather(col_parts, 'row', axis=0, tiled...]
    reshape x3 -> x0, local copies, waits for them, and re-layouts: 8.34 us -> none  [the longest x1 8.15 us: shards(): row_panel = row_panel.reshape(col_count, row_count, local_rows, row_width)]
    slice x0 -> x8, local copies, waits for them, and re-layouts: none -> 7.31 us  [shards(): own = jnp.concatenate([p[:, first:first + size] for p in row_parts], axis=0)]
  transfers between devices with their start and end apart: 2 -> 26, of which waited for: 2 -> 9; matrix products, arithmetic and copies ran while one was open for 4% -> 5% of each run, Pallas kernels for 0% -> 7%
where the time goes in v1:
time: 225 us; the launch traced here: 224 us
  waiting for transfers between devices  140 us (62%)
  starting transfers between devices  37.4 us (17%)
  Pallas kernels  29.8 us (13%)
  local copies, waits for them, and re-layouts  12.4 us (6%)
  other arithmetic  3.78 us (2%)
    ppermute x26, waiting for transfers between devices, send(): return lax.ppermute(value, AXES, flat)  140 us
    ppermute x26, starting transfers between devices, send(): return lax.ppermute(value, AXES, flat)  37.4 us
    pallas_call x2, Pallas kernels, product(): pl.pallas_call(functools.partial(product_kernel, count, first, block is n...  26.9 us
    slice x8, local copies, waits for them, and re-layouts, shards(): own = jnp.concatenate([p[:, first:first + size] for p in row_parts], axis=0)  7.31 us
  transfers between devices with their start and end apart: 26, of which 9 were waited for; matrix products, arithmetic and copies ran while one was open for 5% of the time, Pallas kernels for 7%

profile of v1, /device:TPU:1, one launch (start us, length us, event | category | flops | bytes accessed | tf_op | source)
XLA Modules:
  0.0 223.7 jit_solution(5926100238234789748)
XLA Ops:
  0.0 0.7 stack.62.place
  0.7 2.8 %pick_panels.1 = (bf16[32,4096]{1,0:T(8,128)(2,1)}, bf16[32,4096]{1,0:T(8,128)(2,1)}, bf16[32,4096]{1,0:T(8,128)(2,1)}, bf16[32,4096]{1,0:T(8,128)(2,1)}, bf16[3...) custom-call(s32[8]{0:T(128)} %stack.62.place, ...), custom_call_target="tpu_custom_call" | custom-call | tf_op jit(solution)/shard_map/pick_panels/pallas_call | solution.py:34
  3.5 2.1 collective-permute-start
  5.6 2.3 %collective-permute-start.1 = (bf16[32,4096]{1,0:T(8,128)(2,1)}, bf16[32,4096]{1,0:T(8,128)(2,1)S(1)}, u32[]{:S(2)}, u32[]{:S(2)}) collective-permute-start(bf16[32,4096]{1,0:T(8,128)(2,1)} %get-tuple-element.15), channel_id=1, source_target_pairs={{0,4},{1,5},{2,6},{3,7},{4,0},{5,1},{6,2},{7,3},{8,12},{9,13},{10,... | collective-permute-start | bytes 786440 | tf_op jit(solution)/shard_map/ppermute | solution.py:114
  8.0 1.0 constant_dynamic-update-slice_fusion.3
  8.9 7.8 %collective-permute-done = bf16[32,4096]{1,0:T(8,128)(2,1)S(1)} collective-permute-done((bf16[32,4096]{1,0:T(8,128)(2,1)}, bf16[32,4096]{1,0:T(8,128)(2,1)S(1)}, u32[]{:S(2)}, u32[]{:S(2)}) %collective-permute-start) | collective-permute-done | bytes 262176 | tf_op jit(solution)/shard_map/ppermute | solution.py:114
  16.8 8.2 %collective-permute-done.2 = bf16[32,4096]{1,0:T(8,128)(2,1)S(1)} collective-permute-done((bf16[32,4096]{1,0:T(8,128)(2,1)}, bf16[32,4096]{1,0:T(8,128)(2,1)S(1)}, u32[]{:S(2)}, u32[]{:S(2)}) %collective-permute-start.2) | collective-permute-done | bytes 262176 | tf_op jit(solution)/shard_map/ppermute | solution.py:114
  25.1 2.2 collective-permute-start.5
  27.3 0.2 collective-permute-start.4
  27.5 0.3 collective-permute-start.3
  27.8 1.2 collective-permute-start.7
  29.0 1.2 collective-permute-start.8
  30.2 45.6 %collective-permute-done.7 = bf16[32,4096]{1,0:T(8,128)(2,1)} collective-permute-done((bf16[32,4096]{1,0:T(8,128)(2,1)}, bf16[32,4096]{1,0:T(8,128)(2,1)}, u32[]{:S(2)}, u32[]{:S(2)}) %collective-permute-start.7) | collective-permute-done | bytes 262176 | tf_op jit(solution)/shard_map/ppermute | solution.py:114
  75.8 1.2 collective-permute-start.9
  77.0 0.9 slice.28
  77.9 0.9 slice.35
  78.9 0.4 collective-permute-done.8
  79.3 0.9 slice.36
  80.2 2.1 collective-permute-done.9
  82.3 0.9 slice.37
  83.2 0.0 collective-permute-done.5
  83.2 0.0 collective-permute-done.4
  83.2 1.6 pad_maximum_fusion
  84.9 2.6 %constant_dynamic-slice_fusion.1 = (bf16[512,2048]{1,0:T(8,128)(2,1)}, bf16[512,2048]{1,0:T(8,128)(2,1)}) fusion(bf16[512,4096]{1,0:T(8,128)(2,1)S(1)} %bitcast.29, s32[]{:T(128)S(6)} %select_n.38, s32[]{:T(128)S(6)} %select_n.39), kind=kLoop, calls=%fused_computation.12 | loop fusion | bytes 8388616 | tf_op jit(solution)/shard_map/dynamic_slice | solution.py:138
  87.4 5.8 %collective-permute-start.6 = (bf16[512,2048]{1,0:T(8,128)(2,1)}, bf16[512,2048]{1,0:T(8,128)(2,1)}, u32[]{:S(2)}, u32[]{:S(2)}) collective-permute-start(bf16[512,2048]{1,0:T(8,128)(2,1)} %get-tuple-element.22), channel_id=1, source_target_pairs={{0,1},{1,0},{2,3},{3,2},{4,5},{5,4},{6,7},{7,6},{8,9},{9,8},{10,11... | collective-permute-start | bytes 6291464 | tf_op jit(solution)/shard_map/ppermute | solution.py:114
  93.3 6.2 %collective-permute-start.19 = (bf16[128,2560]{1,0:T(8,128)(2,1)S(1)}, bf16[128,2560]{1,0:T(8,128)(2,1)S(1)}, u32[]{:S(2)}, u32[]{:S(2)}) collective-permute-start(bf16[128,2560]{1,0:T(8,128)(2,1)S(1)} %pad_maximum_fusion.2.refs_0_), channel_id=1, source_target_pairs={{0,4},{1,5},{2,6},{3,7},{4,0},{5,1},{6,2},{7,3},{8,12},{9,13},{10,... | collective-permute-start | bytes 1966088 | tf_op jit(solution)/shard_map/ppermute | solution.py:114
  99.6 0.7 collective-permute-start.20
  100.3 28.5 %collective-permute-done.19.refs_2_ = bf16[128,2560]{1,0:T(8,128)(2,1)S(1)} collective-permute-done((bf16[128,2560]{1,0:T(8,128)(2,1)S(1)}, bf16[128,2560]{1,0:T(8,128)(2,1)S(1)}, u32[]{:S(2)}, u32[]{:S(2)}) %collective-permute-start.19) | collective-permute-done | bytes 655392 | tf_op jit(solution)/shard_map/ppermute | solution.py:114
  128.7 1.3 collective-permute-start.21
  130.0 0.9 slice.24
  130.9 0.9 slice.32
  131.8 0.9 slice.33
  132.7 0.9 slice.34
  133.6 2.1 collective-permute-start.11
  135.7 0.8 dynamic_slice.11
  136.6 0.1 pad_add_fusion.where
  136.6 0.7 collective-permute-start.12
  137.3 22.3 %collective-permute-done.11.refs_2_ = bf16[128,1536]{1,0:T(8,128)(2,1)S(1)} collective-permute-done((bf16[128,1536]{1,0:T(8,128)(2,1)S(1)}, bf16[128,1536]{1,0:T(8,128)(2,1)S(1)}, u32[]{:S(2)}, u32[]{:S(2)}) %collective-permute-start.11) | collective-permute-done | bytes 393248 | tf_op jit(solution)/shard_map/ppermute | solution.py:114
  159.6 0.0 collective-permute-start.10
  159.6 0.0 collective-permute-done.20
  159.6 1.5 collective-permute-start.18
  161.1 0.0 collective-permute-done.21
  161.1 1.3 collective-permute-start.13
  162.4 0.1 broadcast_select_fusion.refs_3_
  162.5 1.4 collective-permute-start.22
  163.9 19.7 %collective-permute-done.18.refs_1_ = bf16[128,2560]{1,0:T(8,128)(2,1)S(1)} collective-permute-done((bf16[128,2560]{1,0:T(8,128)(2,1)S(1)}, bf16[128,2560]{1,0:T(8,128)(2,1)S(1)}, u32[]{:S(2)}, u32[]{:S(2)}) %collective-permute-start.18) | collective-permute-done | bytes 655392 | tf_op jit(solution)/shard_map/ppermute | solution.py:114
  183.5 2.9 %collective-permute-start.24 = (bf16[128,2560]{1,0:T(8,128)(2,1)S(1)}, bf16[128,2560]{1,0:T(8,128)(2,1)S(1)}, u32[]{:S(2)}, u32[]{:S(2)}) collective-permute-start(bf16[128,2560]{1,0:T(8,128)(2,1)S(1)} %collective-permute-done.19.refs_2_), channel_id=1, source_target_pairs={{0,1},{1,0},{2,3},{3,2},{4,5},{5,4},{6,7},{7,6},{8,9},{9,8},{10,11... | collective-permute-start | bytes 1966088 | tf_op jit(solution)/shard_map/ppermute | solution.py:114
  186.4 5.5 %collective-permute-done.13 = bf16[128,1536]{1,0:T(8,128)(2,1)S(1)} collective-permute-done((bf16[128,1536]{1,0:T(8,128)(2,1)S(1)}, bf16[128,1536]{1,0:T(8,128)(2,1)S(1)}, u32[]{:S(2)}, u32[]{:S(2)}) %collective-permute-start.13) | collective-permute-done | bytes 393248 | tf_op jit(solution)/shard_map/ppermute | solution.py:114
  192.0 1.6 collective-permute-start.23
  193.6 0.0 collective-permute-done.6
  193.6 0.0 collective-permute-start.25
  193.7 1.9 pad_maximum_fusion.1.col
  195.6 0.0 collective-permute-done.10.refs_1_
  195.6 0.6 collective-permute-start.14
  196.2 0.0 collective-permute-done.22.refs_4_
  196.2 0.1 collective-permute-start.16
  196.3 0.4 collective-permute-start.15
  196.7 0.0 collective-permute-done.23.refs_5_
  196.7 0.1 collective-permute-start.17
  196.8 15.5 %product.2.refs_8_ = f32[4096,2048]{1,0:T(8,128)} custom-call(s32[2]{0:T(128)S(1)} %pad_add_fusion.where, bf16[1024,2048]{1,0:T(8,128)(2,1)S(1)} %pad_maximum_fusion.1.col, f32[1,2048]{1,0:T(1,128)S(1)} %bitcast.27, bf16[128,2560]{1,0:T(8,128)(2,1)S(1)} %pad_maximum_fusion.2.refs_0_, bf16[128,2560]{1,0:T(8,128)(2,1)S(1)} %collective-permute-done.18.refs_1_, ...), custom_call_target="tpu_custom_call" | custom-call | flops 10737418240 | bytes 30408704 | tf_op jit(solution)/shard_map/product/pallas_call | solution.py:83
  212.3 0.0 collective-permute-done.14.refs_4_
  212.3 0.0 collective-permute-done.16.refs_6_
  212.3 0.0 collective-permute-done.15.refs_5_
  212.3 11.4 %product.3 = f32[4096,2048]{1,0:T(8,128)} custom-call(s32[2]{0:T(128)S(1)} %pad_add_fusion.where, bf16[1024,2048]{1,0:T(8,128)(2,1)S(1)} %pad_maximum_fusion.1.col, f32[1,2048]{1,0:T(1,128)S(1)} %bitcast.28, bf16[128,1536]{1,0:T(8,128)(2,1)S(1)} %pad_maximum_fusion.3.refs_0_, ...), custom_call_target="tpu_custom_call", output_to_operand_aliasing={{}: (11, {})} | custom-call | flops 6442450944 | bytes 19922944 | tf_op jit(solution)/shard_map/product/pallas_call | solution.py:83
  (15 shorter events, 0.2 us)
Async XLA Ops:
  3.5 13.2 %collective-permute-start = (bf16[32,4096]{1,0:T(8,128)(2,1)}, bf16[32,4096]{1,0:T(8,128)(2,1)S(1)}, u32[]{:S(2)}, u32[]{:S(2)}) collective-permute-start(bf16[32,4096]{1,0:T(8,128)(2,1)} %get-tuple-element.14), channel_id=1, source_target_pairs={{0,2},{1,3},{2,0},{3,1},{4,6},{5,7},{6,4},{7,5},{8,10},{9,11},{10,... | collective-permute-start | bytes 786440 | tf_op jit(solution)/shard_map/ppermute | solution.py:114
  5.6 11.1 %collective-permute-start.1 = (bf16[32,4096]{1,0:T(8,128)(2,1)}, bf16[32,4096]{1,0:T(8,128)(2,1)S(1)}, u32[]{:S(2)}, u32[]{:S(2)}) collective-permute-start(bf16[32,4096]{1,0:T(8,128)(2,1)} %get-tuple-element.15), channel_id=1, source_target_pairs={{0,4},{1,5},{2,6},{3,7},{4,0},{5,1},{6,2},{7,3},{8,12},{9,13},{10,... | collective-permute-start | bytes 786440 | tf_op jit(solution)/shard_map/ppermute | solution.py:114
  8.0 17.1 %collective-permute-start.2 = (bf16[32,4096]{1,0:T(8,128)(2,1)}, bf16[32,4096]{1,0:T(8,128)(2,1)S(1)}, u32[]{:S(2)}, u32[]{:S(2)}) collective-permute-start(bf16[32,4096]{1,0:T(8,128)(2,1)} %get-tuple-element.16), channel_id=1, source_target_pairs={{0,6},{1,7},{2,4},{3,5},{4,2},{5,3},{6,0},{7,1},{8,14},{9,15},{10,... | collective-permute-start | bytes 786440 | tf_op jit(solution)/shard_map/ppermute | solution.py:114
  25.1 58.2 %collective-permute-start.5 = (bf16[128,4096]{1,0:T(8,128)(2,1)S(1)}, bf16[128,4096]{1,0:T(8,128)(2,1)S(1)}, u32[]{:S(2)}, u32[]{:S(2)}) collective-permute-start(bf16[128,4096]{1,0:T(8,128)(2,1)S(1)} %constant_dynamic-update-slice_fusion), channel_id=1, source_target_pairs={{0,24},{1,25},{2,26},{3,27},{4,28},{5,29},{6,30},{7,31},{8,16},{9,... | collective-permute-start | bytes 3145736 | tf_op jit(solution)/shard_map/ppermute | solution.py:114
  27.3 55.9 %collective-permute-start.4 = (bf16[128,4096]{1,0:T(8,128)(2,1)S(1)}, bf16[128,4096]{1,0:T(8,128)(2,1)S(1)}, u32[]{:S(2)}, u32[]{:S(2)}) collective-permute-start(bf16[128,4096]{1,0:T(8,128)(2,1)S(1)} %constant_dynamic-update-slice_fusion), channel_id=1, source_target_pairs={{0,16},{1,17},{2,18},{3,19},{4,20},{5,21},{6,22},{7,23},{8,24},{9,... | collective-permute-start | bytes 3145736 | tf_op jit(solution)/shard_map/ppermute | solution.py:114
  27.5 55.7 %collective-permute-start.3 = (bf16[128,4096]{1,0:T(8,128)(2,1)S(1)}, bf16[128,4096]{1,0:T(8,128)(2,1)}, u32[]{:S(2)}, u32[]{:S(2)}) collective-permute-start(bf16[128,4096]{1,0:T(8,128)(2,1)S(1)} %constant_dynamic-update-slice_fusion), channel_id=1, source_target_pairs={{0,8},{1,9},{2,10},{3,11},{4,12},{5,13},{6,14},{7,15},{8,0},{9,1},... | collective-permute-start | bytes 3145736 | tf_op jit(solution)/shard_map/ppermute | solution.py:114
  27.8 48.1 %collective-permute-start.7 = (bf16[32,4096]{1,0:T(8,128)(2,1)}, bf16[32,4096]{1,0:T(8,128)(2,1)}, u32[]{:S(2)}, u32[]{:S(2)}) collective-permute-start(bf16[32,4096]{1,0:T(8,128)(2,1)} %get-tuple-element.18), channel_id=1, source_target_pairs={{0,8},{1,9},{2,10},{3,11},{4,12},{5,13},{6,14},{7,15},{8,0},{9,1},... | collective-permute-start | bytes 786440 | tf_op jit(solution)/shard_map/ppermute | solution.py:114
  29.0 50.3 %collective-permute-start.8 = (bf16[32,4096]{1,0:T(8,128)(2,1)}, bf16[32,4096]{1,0:T(8,128)(2,1)}, u32[]{:S(2)}, u32[]{:S(2)}) collective-permute-start(bf16[32,4096]{1,0:T(8,128)(2,1)} %get-tuple-element.19), channel_id=1, source_target_pairs={{0,16},{1,17},{2,18},{3,19},{4,20},{5,21},{6,22},{7,23},{8,24},{9,... | collective-permute-start | bytes 786440 | tf_op jit(solution)/shard_map/ppermute | solution.py:114
  75.8 6.4 %collective-permute-start.9 = (bf16[32,4096]{1,0:T(8,128)(2,1)}, bf16[32,4096]{1,0:T(8,128)(2,1)}, u32[]{:S(2)}, u32[]{:S(2)}) collective-permute-start(bf16[32,4096]{1,0:T(8,128)(2,1)} %get-tuple-element.20), channel_id=1, source_target_pairs={{0,24},{1,25},{2,26},{3,27},{4,28},{5,29},{6,30},{7,31},{8,16},{9,... | collective-permute-start | bytes 786440 | tf_op jit(solution)/shard_map/ppermute | solution.py:114
  87.4 106.2 %collective-permute-start.6 = (bf16[512,2048]{1,0:T(8,128)(2,1)}, bf16[512,2048]{1,0:T(8,128)(2,1)}, u32[]{:S(2)}, u32[]{:S(2)}) collective-permute-start(bf16[512,2048]{1,0:T(8,128)(2,1)} %get-tuple-element.22), channel_id=1, source_target_pairs={{0,1},{1,0},{2,3},{3,2},{4,5},{5,4},{6,7},{7,6},{8,9},{9,8},{10,11... | collective-permute-start | bytes 6291464 | tf_op jit(solution)/shard_map/ppermute | solution.py:114
  93.3 35.4 %collective-permute-start.19 = (bf16[128,2560]{1,0:T(8,128)(2,1)S(1)}, bf16[128,2560]{1,0:T(8,128)(2,1)S(1)}, u32[]{:S(2)}, u32[]{:S(2)}) collective-permute-start(bf16[128,2560]{1,0:T(8,128)(2,1)S(1)} %pad_maximum_fusion.2.refs_0_), channel_id=1, source_target_pairs={{0,4},{1,5},{2,6},{3,7},{4,0},{5,1},{6,2},{7,3},{8,12},{9,13},{10,... | collective-permute-start | bytes 1966088 | tf_op jit(solution)/shard_map/ppermute | solution.py:114
  99.6 60.1 %collective-permute-start.20 = (bf16[128,2560]{1,0:T(8,128)(2,1)S(1)}, bf16[128,2560]{1,0:T(8,128)(2,1)S(1)}, u32[]{:S(2)}, u32[]{:S(2)}) collective-permute-start(bf16[128,2560]{1,0:T(8,128)(2,1)S(1)} %pad_maximum_fusion.2.refs_0_), channel_id=1, source_target_pairs={{2,4},{3,5},{4,2},{5,3},{10,12},{11,13},{12,10},{13,11},{18,20},{1... | collective-permute-start | bytes 1966088 | tf_op jit(solution)/shard_map/ppermute | solution.py:114
  128.7 32.4 %collective-permute-start.21 = (bf16[128,2560]{1,0:T(8,128)(2,1)S(1)}, bf16[128,2560]{1,0:T(8,128)(2,1)S(1)}, u32[]{:S(2)}, u32[]{:S(2)}) collective-permute-start(bf16[128,2560]{1,0:T(8,128)(2,1)S(1)} %collective-permute-done.19.refs_2_), channel_id=1, source_target_pairs={{2,0},{3,1},{4,6},{5,7},{10,8},{11,9},{12,14},{13,15},{18,16},{19,... | collective-permute-start | bytes 1966088 | tf_op jit(solution)/shard_map/ppermute | solution.py:114
  133.6 26.0 %collective-permute-start.11 = (bf16[128,1536]{1,0:T(8,128)(2,1)S(1)}, bf16[128,1536]{1,0:T(8,128)(2,1)S(1)}, u32[]{:S(2)}, u32[]{:S(2)}) collective-permute-start(bf16[128,1536]{1,0:T(8,128)(2,1)S(1)} %pad_maximum_fusion.3.refs_0_), channel_id=1, source_target_pairs={{0,4},{1,5},{2,6},{3,7},{4,0},{5,1},{6,2},{7,3},{8,12},{9,13},{10,... | collective-permute-start | bytes 1179656 | tf_op jit(solution)/shard_map/ppermute | solution.py:114
  135.7 58.0 %copy-start = (bf16[512,2048]{1,0:T(8,128)(2,1)S(1)}, bf16[512,2048]{1,0:T(8,128)(2,1)}, u32[]{:S(2)}) copy-start(bf16[512,2048]{1,0:T(8,128)(2,1)} %get-tuple-element.21) | copy-start | bytes 6291460
  136.6 25.8 %collective-permute-start.12 = (bf16[128,1536]{1,0:T(8,128)(2,1)S(1)}, bf16[128,1536]{1,0:T(8,128)(2,1)S(1)}, u32[]{:S(2)}, u32[]{:S(2)}) collective-permute-start(bf16[128,1536]{1,0:T(8,128)(2,1)S(1)} %pad_maximum_fusion.3.refs_0_), channel_id=1, source_target_pairs={{2,4},{3,5},{4,2},{5,3},{10,12},{11,13},{12,10},{13,11},{18,20},{1... | collective-permute-start | bytes 1179656 | tf_op jit(solution)/shard_map/ppermute | solution.py:114
  159.6 36.0 %collective-permute-start.10 = (bf16[128,1536]{1,0:T(8,128)(2,1)S(1)}, bf16[128,1536]{1,0:T(8,128)(2,1)S(1)}, u32[]{:S(2)}, u32[]{:S(2)}) collective-permute-start(bf16[128,1536]{1,0:T(8,128)(2,1)S(1)} %pad_maximum_fusion.3.refs_0_), channel_id=1, source_target_pairs={{0,2},{1,3},{2,0},{3,1},{4,6},{5,7},{6,4},{7,5},{8,10},{9,11},{10,... | collective-permute-start | bytes 1179656 | tf_op jit(solution)/shard_map/ppermute | solution.py:114
  159.6 23.9 %collective-permute-start.18 = (bf16[128,2560]{1,0:T(8,128)(2,1)S(1)}, bf16[128,2560]{1,0:T(8,128)(2,1)S(1)}, u32[]{:S(2)}, u32[]{:S(2)}) collective-permute-start(bf16[128,2560]{1,0:T(8,128)(2,1)S(1)} %pad_maximum_fusion.2.refs_0_), channel_id=1, source_target_pairs={{0,2},{1,3},{2,0},{3,1},{4,6},{5,7},{6,4},{7,5},{8,10},{9,11},{10,... | collective-permute-start | bytes 1966088 | tf_op jit(solution)/shard_map/ppermute | solution.py:114
  161.1 30.9 %collective-permute-start.13 = (bf16[128,1536]{1,0:T(8,128)(2,1)S(1)}, bf16[128,1536]{1,0:T(8,128)(2,1)S(1)}, u32[]{:S(2)}, u32[]{:S(2)}) collective-permute-start(bf16[128,1536]{1,0:T(8,128)(2,1)S(1)} %collective-permute-done.11.refs_2_), channel_id=1, source_target_pairs={{2,0},{3,1},{4,6},{5,7},{10,8},{11,9},{12,14},{13,15},{18,16},{19,... | collective-permute-start | bytes 1179656 | tf_op jit(solution)/shard_map/ppermute | solution.py:114
  162.5 33.7 %collective-permute-start.22 = (bf16[128,2560]{1,0:T(8,128)(2,1)S(1)}, bf16[128,2560]{1,0:T(8,128)(2,1)S(1)}, u32[]{:S(2)}, u32[]{:S(2)}) collective-permute-start(bf16[128,2560]{1,0:T(8,128)(2,1)S(1)} %pad_maximum_fusion.2.refs_0_), channel_id=1, source_target_pairs={{0,1},{1,0},{2,3},{3,2},{4,5},{5,4},{6,7},{7,6},{8,9},{9,8},{10,11... | collective-permute-start | bytes 1966088 | tf_op jit(solution)/shard_map/ppermute | solution.py:114
  183.5 12.7 %collective-permute-start.24 = (bf16[128,2560]{1,0:T(8,128)(2,1)S(1)}, bf16[128,2560]{1,0:T(8,128)(2,1)S(1)}, u32[]{:S(2)}, u32[]{:S(2)}) collective-permute-start(bf16[128,2560]{1,0:T(8,128)(2,1)S(1)} %collective-permute-done.19.refs_2_), channel_id=1, source_target_pairs={{0,1},{1,0},{2,3},{3,2},{4,5},{5,4},{6,7},{7,6},{8,9},{9,8},{10,11... | collective-permute-start | bytes 1966088 | tf_op jit(solution)/shard_map/ppermute | solution.py:114
  192.0 4.7 %collective-permute-start.23 = (bf16[128,2560]{1,0:T(8,128)(2,1)S(1)}, bf16[128,2560]{1,0:T(8,128)(2,1)S(1)}, u32[]{:S(2)}, u32[]{:S(2)}) collective-permute-start(bf16[128,2560]{1,0:T(8,128)(2,1)S(1)} %collective-permute-done.18.refs_1_), channel_id=1, source_target_pairs={{0,1},{1,0},{2,3},{3,2},{4,5},{5,4},{6,7},{7,6},{8,9},{9,8},{10,11... | collective-permute-start | bytes 1966088 | tf_op jit(solution)/shard_map/ppermute | solution.py:114
  193.6 3.2 %collective-permute-start.25 = (bf16[128,2560]{1,0:T(8,128)(2,1)S(1)}, bf16[128,2560]{1,0:T(8,128)(2,1)S(1)}, u32[]{:S(2)}, u32[]{:S(2)}) collective-permute-start(bf16[128,2560]{1,0:T(8,128)(2,1)S(1)} %broadcast_select_fusion.refs_3_), channel_id=1, source_target_pairs={{0,1},{1,0},{2,3},{3,2},{4,5},{5,4},{6,7},{7,6},{8,9},{9,8},{10,11... | collective-permute-start | bytes 1966088 | tf_op jit(solution)/shard_map/ppermute | solution.py:114
  195.6 16.7 %collective-permute-start.14 = (bf16[128,1536]{1,0:T(8,128)(2,1)S(1)}, bf16[128,1536]{1,0:T(8,128)(2,1)S(1)}, u32[]{:S(2)}, u32[]{:S(2)}) collective-permute-start(bf16[128,1536]{1,0:T(8,128)(2,1)S(1)} %pad_maximum_fusion.3.refs_0_), channel_id=1, source_target_pairs={{0,1},{1,0},{2,3},{3,2},{4,5},{5,4},{6,7},{7,6},{8,9},{9,8},{10,11... | collective-permute-start | bytes 1179656 | tf_op jit(solution)/shard_map/ppermute | solution.py:114
  196.2 16.1 %collective-permute-start.16 = (bf16[128,1536]{1,0:T(8,128)(2,1)S(1)}, bf16[128,1536]{1,0:T(8,128)(2,1)S(1)}, u32[]{:S(2)}, u32[]{:S(2)}) collective-permute-start(bf16[128,1536]{1,0:T(8,128)(2,1)S(1)} %collective-permute-done.11.refs_2_), channel_id=1, source_target_pairs={{0,1},{1,0},{2,3},{3,2},{4,5},{5,4},{6,7},{7,6},{8,9},{9,8},{10,11... | collective-permute-start | bytes 1179656 | tf_op jit(solution)/shard_map/ppermute | solution.py:114
  196.3 16.1 %collective-permute-start.15 = (bf16[128,1536]{1,0:T(8,128)(2,1)S(1)}, bf16[128,1536]{1,0:T(8,128)(2,1)S(1)}, u32[]{:S(2)}, u32[]{:S(2)}) collective-permute-start(bf16[128,1536]{1,0:T(8,128)(2,1)S(1)} %collective-permute-done.10.refs_1_), channel_id=1, source_target_pairs={{0,1},{1,0},{2,3},{3,2},{4,5},{5,4},{6,7},{7,6},{8,9},{9,8},{10,11... | collective-permute-start | bytes 1179656 | tf_op jit(solution)/shard_map/ppermute | solution.py:114
  196.7 15.6 %collective-permute-start.17 = (bf16[128,1536]{1,0:T(8,128)(2,1)S(1)}, bf16[128,1536]{1,0:T(8,128)(2,1)S(1)}, u32[]{:S(2)}, u32[]{:S(2)}) collective-permute-start(bf16[128,1536]{1,0:T(8,128)(2,1)S(1)} %broadcast_select_fusion.1.refs_3_), channel_id=1, source_target_pairs={{0,1},{1,0},{2,3},{3,2},{4,5},{5,4},{6,7},{7,6},{8,9},{9,8},{10,11... | collective-permute-start | bytes 1179656 | tf_op jit(solution)/shard_map/ppermute | solution.py:114

commit v2 on v1

v2 whole, which is shorter than its diff:
```python
import functools
import math

import jax
import jax.numpy as jnp
from jax import lax
from jax.experimental import pallas as pl
from jax.experimental.pallas import tpu as pltpu
from jax.sharding import PartitionSpec as P

AXES = ("row", "col")
CORES = 2
CHUNKS = (16, 16)
BLOCK_ROWS = 512


def after(value, *others):
    return lax.optimization_barrier((value,) + others)[0]


def pick_kernel(lines, mask, slab, *outs):
    line = lax.axis_index("row")
    plane = lax.axis_index("col") // CORES
    span = slab.shape[1] // mask.shape[1]
    for slot, out in enumerate(outs):
        width = out.shape[1]
        step = min(width, span)
        panel = line ^ slot if slot < lines else plane ^ (slot - lines)
        for part in range(width // step):
            start = pl.multiple_of(panel * width + part * step, step)
            keep = mask[0, start // span]
            piece = slab[:, pl.ds(start, step)]
            out[:, part * step : (part + 1) * step] = jnp.where(keep != 0, piece, jnp.zeros_like(piece))


def pick_panels(slab, mask, lines, planes):
    rows, width = slab.shape
    return pl.pallas_call(
        functools.partial(pick_kernel, lines),
        out_shape=[jax.ShapeDtypeStruct((rows, width // lines), slab.dtype)] * (lines + planes),
        in_specs=[
            pl.BlockSpec(memory_space=pltpu.SMEM),
            pl.BlockSpec(memory_space=pltpu.VMEM),
        ],
        out_specs=[pl.BlockSpec(memory_space=pltpu.VMEM)] * (lines + planes),
        name="pick_panels",
    )(mask, slab)


def product_kernel(count, lines, total, first, col, damp, *refs):
    parts = refs[:count]
    out = refs[-1]
    step = pl.program_id(0)
    rows, cols = out.shape
    group = parts[0].shape[0] // lines
    left = jnp.concatenate(
        [part[m * group : (m + 1) * group, :] for m in range(lines) for part in parts], axis=0
    )
    out[...] = lax.dot_general(
        left, col[...], (((0,), (0,)), ((), ())), preferred_element_type=jnp.float32
    )
    row_at = lax.axis_index("row") * total + first + step * rows
    col_at = lax.axis_index("col") * cols

    @pl.when((row_at < col_at + cols) & (col_at < row_at + rows))
    def _():
        row_ids = lax.broadcasted_iota(jnp.int32, (rows, cols), 0) + row_at
        col_ids = lax.broadcasted_iota(jnp.int32, (rows, cols), 1) + col_at
        mine = damp[:, pl.ds(pl.multiple_of(col_at, cols), cols)]
        out[...] += jnp.where(row_ids == col_ids, mine, 0.0)


def product(parts, col, damp, lines, total, first, width, block):
    depth = parts[0].shape[0]
    rows = math.gcd(BLOCK_ROWS, width, first)
    steps = width // rows
    held, cols = col.shape
    count = len(parts)
    return pl.pallas_call(
        functools.partial(product_kernel, count, lines, total, first),
        out_shape=jax.ShapeDtypeStruct((total, cols), jnp.float32),
        grid=(steps,),
        in_specs=[
            pl.BlockSpec((held, cols), lambda i: (0, 0)),
            pl.BlockSpec(damp.shape, lambda i: (0, 0)),
        ]
        + [
            pl.BlockSpec((depth, rows), lambda i, at=first // rows if p.shape[1] == total else 0: (0, at + i))
            for p in parts
        ]
        + ([] if block is None else [pl.BlockSpec(memory_space=pl.ANY)]),
        out_specs=pl.BlockSpec((rows, cols), lambda i: (first // rows + i, 0)),
        input_output_aliases={} if block is None else {2 + count: 0},
        compiler_params=pltpu.CompilerParams(vmem_limit_bytes=40 << 20),
        cost_estimate=pl.CostEstimate(flops=0, bytes_accessed=0, transcendentals=0),
        name="product",
    )(col, damp, *parts, *([] if block is None else [block]))


def shards(slab, block_mask, damping):
    lines = lax.axis_size("row")
    cols = lax.axis_size("col")
    planes = cols // CORES
    group, width = slab.shape
    panel = width // lines
    half = width // cols
    line = lax.axis_index("row")
    place = lax.axis_index("col")
    plane = place // CORES
    core = place % CORES

    everyone = [(r, q, c) for r in range(lines) for q in range(planes) for c in range(CORES)]

    def send(value, to):
        flat = []
        for r, q, c in everyone:
            target = to(r, q, c)
            if target is not None:
                r1, q1, c1 = target
                flat.append(((r * planes + q) * CORES + c, (r1 * planes + q1) * CORES + c1))
        return lax.ppermute(value, AXES, flat)

    def across_lines(value, m):
        return send(value, lambda r, q, c: (r ^ m, q, c))

    def across_planes(value, k):
        return send(value, lambda r, q, c: (r, q ^ k, c))

    def across_cores(value):
        return send(value, lambda r, q, c: (r, q, 1 - c))

    def swap_inner(value):
        return send(value, lambda r, q, c: (r, q ^ 3, c) if q in (1, 2) else None)

    def push_out(value):
        return send(value, lambda r, q, c: (r, q ^ 1, c) if q in (1, 2) else None)

    picked = pick_panels(slab, block_mask, lines, planes)
    by_line, by_plane = picked[:lines], picked[lines:]

    row_parts = [by_line[0]] + [across_lines(by_line[m], m) for m in range(1, lines)]
    col_parts = [by_plane[0]]
    for k in range(1, planes):
        col_parts.append(across_planes(after(by_plane[k], row_parts[1]) if k == 1 else by_plane[k], k))
    mine = jnp.concatenate(col_parts, axis=0)
    keep = lax.dynamic_slice_in_dim(mine, core * half, half, 1)
    give = lax.dynamic_slice_in_dim(mine, (1 - core) * half, half, 1)
    mine = jnp.concatenate([keep, across_cores(give)], axis=0)
    own = jnp.concatenate(row_parts, axis=0)

    share = panel // sum(CHUNKS)
    cuts = [0]
    for chunk in CHUNKS:
        cuts.append(cuts[-1] + chunk * share)

    def cut(value):
        return [value[:, i:j] for i, j in zip(cuts, cuts[1:])]

    if planes == 4 and lines == 4:
        inner = (plane == 1) | (plane == 2)
        near = across_planes(own, 1)
        mid = swap_inner(own)
        col_lines = [mine, across_lines(mine, 1), across_lines(mine, 2)]
        one, two = col_lines[1:]
        near, mid = lax.optimization_barrier((near, mid))
        far_in = swap_inner(near)
        far_out = push_out(mid)
        third = across_lines(after(mine, near, mid, one, two), 3)
        held = jnp.concatenate([mine, one, two], axis=0)
        far_in, far_out, third, held = lax.optimization_barrier((far_in, far_out, third, held))
        col_panel = jnp.concatenate([held, third], axis=0)
        last = []
        for piece in cut(far_in):
            last.append(push_out(after(piece, *last, *([col_panel] if last else []))))
        far = jnp.where(inner, far_in, far_out)
        across = [across_cores(p) for p in (own, near, far)]
        split = list(zip(cut(mid), last))
        full = [own, near, far] + across
    else:
        col_lines = [mine] + [across_lines(mine, m) for m in range(1, lines)]
        full = [own] + [across_planes(own, k) for k in range(1, planes)]
        full += [across_cores(p) for p in full]
        split = [None] * len(CHUNKS)
        col_panel = jnp.concatenate(col_lines, axis=0)

    out = None
    for first, end, pair in zip(cuts, cuts[1:], split):
        parts = full
        if pair is not None:
            middle, outer = pair
            if out is not None:
                outer, out = lax.optimization_barrier((outer, out))
            part = jnp.where(inner, middle, outer)
            at = len(full) // 2
            parts = full[:at] + [part] + full[at:] + [across_cores(part)]
        out = product(parts, col_panel, damping[None, :], lines, panel, first, end - first, out)
    return out


def solution(mesh):
    placed = (P(("row", "col"), None), P(("row", "col"), None), P())
    return jax.shard_map(
        shards, mesh=mesh, in_specs=placed, out_specs=P("row", "col"), check_vma=False
    )
```

time: 225 us -> 143 us (0.64)
  waiting for transfers between devices: 140 us -> 68 us
  local copies, waits for them, and re-layouts: 12.4 us -> 6.14 us
  starting transfers between devices: 37.4 us -> 33.8 us
  other arithmetic: 3.78 us -> 6.27 us
    ppermute x26 -> x21, waiting for transfers between devices: 140 us -> 68 us  [send(): return lax.ppermute(value, AXES, flat)]
    slice x8 -> x1, local copies, waits for them, and re-layouts: 7.31 us -> 1.3 us  [cut(): return [value[:, i:j] for i, j in zip(cuts, cuts[1:])]]
    ppermute x26 -> x21, starting transfers between devices: 37.4 us -> 33.8 us  [send(): return lax.ppermute(value, AXES, flat)]
    select_n x2 -> x3, other arithmetic: 0.12 us -> 3.55 us  [the longest x2 2.2 us: shards(): part = jnp.where(inner, middle, outer)]
    dynamic_slice x2 -> x1, local copies, waits for them, and re-layouts: 3.42 us -> 0.11 us  [shards(): keep = lax.dynamic_slice_in_dim(mine, core * half, half, 1)]
    unnamed x5 -> x9, local copies, waits for them, and re-layouts: 1.01 us -> 3.37 us
  transfers between devices with their start and end apart: 26 -> 21, of which waited for: 9 -> 8; matrix products, arithmetic and copies ran while one was open for 5% -> 8% of each run, Pallas kernels for 7% -> 8%
where the time goes in v2:
time: 143 us
  waiting for transfers between devices  68 us (48%)
  starting transfers between devices  33.8 us (24%)
  Pallas kernels  28.4 us (20%)
  other arithmetic  6.27 us (4%)
  local copies, waits for them, and re-layouts  6.14 us (4%)
    ppermute x21, waiting for transfers between devices, send(): return lax.ppermute(value, AXES, flat)  68 us
    ppermute x21, starting transfers between devices, send(): return lax.ppermute(value, AXES, flat)  33.8 us
    pallas_call x2, Pallas kernels, product(): pl.pallas_call(functools.partial(product_kernel, count, lines, total, fir...  25.7 us
    unnamed x9, local copies, waits for them, and re-layouts  3.37 us
  transfers between devices with their start and end apart: 21, of which 8 were waited for; matrix products, arithmetic and copies ran while one was open for 8% of the time, Pallas kernels for 8%

profile of v2, /device:TPU:1, one launch (start us, length us, event | category | flops | bytes accessed | tf_op | source)
XLA Modules:
  0.0 142.8 jit_solution(2321043932362674452)
XLA Ops:
  0.0 2.8 %pick_panels.1 = (bf16[32,4096]{1,0:T(8,128)(2,1)}, bf16[32,4096]{1,0:T(8,128)(2,1)}, bf16[32,4096]{1,0:T(8,128)(2,1)}, bf16[32,4096]{1,0:T(8,128)(2,1)}, bf16[3...) custom-call(s32[1,16]{1,0:T(1,128)} %mask.1, ...), custom_call_target="tpu_custom_call" | custom-call | tf_op jit(solution)/shard_map/pick_panels/pallas_call | solution.py:38
  2.8 2.0 %collective-permute-start = (bf16[32,4096]{1,0:T(8,128)(2,1)}, bf16[32,4096]{1,0:T(8,128)(2,1)S(1)}, u32[]{:S(2)}, u32[]{:S(2)}) collective-permute-start(bf16[32,4096]{1,0:T(8,128)(2,1)} %get-tuple-element.25), channel_id=1, source_target_pairs={{0,8},{1,9},{2,10},{3,11},{4,12},{5,13},{6,14},{7,15},{8,0},{9,1},... | collective-permute-start | bytes 786440 | tf_op jit(solution)/shard_map/ppermute | solution.py:121
  4.8 1.2 collective-permute-start.1
  6.1 0.0 collective-permute-start.2
  6.1 2.5 %collective-permute-start.8 = (bf16[32,4096]{1,0:T(8,128)(2,1)}, bf16[32,4096]{1,0:T(8,128)(2,1)S(1)}, u32[]{:S(2)}, u32[]{:S(2)}) collective-permute-start(bf16[32,4096]{1,0:T(8,128)(2,1)} %get-tuple-element.33), channel_id=1, source_target_pairs={{0,4},{1,5},{2,6},{3,7},{4,0},{5,1},{6,2},{7,3},{8,12},{9,13},{10,... | collective-permute-start | bytes 786440 | tf_op jit(solution)/shard_map/ppermute | solution.py:121
  8.6 1.1 collective-permute-start.9
  9.6 1.0 constant_dynamic-update-slice_fusion.3
  10.6 1.0 constant_dynamic-update-slice_fusion.7
  11.6 0.0 collective-permute-done
  11.6 0.8 collective-permute-start.7
  12.4 16.4 %collective-permute-done.7 = bf16[32,4096]{1,0:T(8,128)(2,1)S(1)} collective-permute-done((bf16[32,4096]{1,0:T(8,128)(2,1)}, bf16[32,4096]{1,0:T(8,128)(2,1)S(1)}, u32[]{:S(2)}, u32[]{:S(2)}) %collective-permute-start.7) | collective-permute-done | bytes 262176 | tf_op jit(solution)/shard_map/ppermute | solution.py:121
  28.8 0.0 collective-permute-done.8
  28.9 0.0 collective-permute-done.9
  28.9 0.1 constant_dynamic-slice_fusion.1
  29.0 1.9 %collective-permute-start.10 = (bf16[128,2048]{1,0:T(8,128)(2,1)S(1)}, bf16[128,2048]{1,0:T(8,128)(2,1)S(1)}, u32[]{:S(2)}, u32[]{:S(2)}) collective-permute-start(bf16[128,2048]{1,0:T(8,128)(2,1)S(1)} %get-tuple-element.46), channel_id=1, source_target_pairs={{0,1},{1,0},{2,3},{3,2},{4,5},{5,4},{6,7},{7,6},{8,9},{9,8},{10,11... | collective-permute-start | bytes 1572872 | tf_op jit(solution)/shard_map/ppermute | solution.py:121
  30.9 0.0 collective-permute-done.1
  30.9 1.0 constant_dynamic-update-slice_fusion.1
  31.9 0.0 collective-permute-done.2
  32.0 1.7 %collective-permute-start.4 = (bf16[128,4096]{1,0:T(8,128)(2,1)S(1)}, bf16[128,4096]{1,0:T(8,128)(2,1)}, u32[]{:S(2)}, u32[]{:S(2)}) collective-permute-start(bf16[128,4096]{1,0:T(8,128)(2,1)S(1)} %constant_dynamic-update-slice_fusion.refs_0_), channel_id=1, source_target_pairs={{2,4},{3,5},{4,2},{5,3},{10,12},{11,13},{12,10},{13,11},{18,20},{1... | collective-permute-start | bytes 3145736 | tf_op jit(solution)/shard_map/ppermute | solution.py:121
  33.6 5.2 %collective-permute-start.3 = (bf16[128,4096]{1,0:T(8,128)(2,1)S(1)}, bf16[128,4096]{1,0:T(8,128)(2,1)S(1)}, u32[]{:S(2)}, u32[]{:S(2)}) collective-permute-start(bf16[128,4096]{1,0:T(8,128)(2,1)S(1)} %constant_dynamic-update-slice_fusion.refs_0_), channel_id=1, source_target_pairs={{0,2},{1,3},{2,0},{3,1},{4,6},{5,7},{6,4},{7,5},{8,10},{9,11},{10,... | collective-permute-start | bytes 3145736 | tf_op jit(solution)/shard_map/ppermute | solution.py:121
  38.8 0.0 collective-permute-done.10
  38.8 1.0 pad_maximum_fusion.1
  39.8 1.2 collective-permute-start.12
  41.1 1.2 collective-permute-start.11
  42.3 0.0 collective-permute-done.4
  42.3 19.9 %collective-permute-done.3.refs_1_ = bf16[128,4096]{1,0:T(8,128)(2,1)S(1)} collective-permute-done((bf16[128,4096]{1,0:T(8,128)(2,1)S(1)}, bf16[128,4096]{1,0:T(8,128)(2,1)S(1)}, u32[]{:S(2)}, u32[]{:S(2)}) %collective-permute-start.3) | collective-permute-done | bytes 1048608 | tf_op jit(solution)/shard_map/ppermute | solution.py:121
  62.2 1.3 collective-permute-start.6
  63.5 1.7 %collective-permute-start.5 = (bf16[128,4096]{1,0:T(8,128)(2,1)S(1)}, bf16[128,4096]{1,0:T(8,128)(2,1)}, u32[]{:S(2)}, u32[]{:S(2)}) collective-permute-start(bf16[128,4096]{1,0:T(8,128)(2,1)S(1)} %collective-permute-done.3.refs_1_), channel_id=1, source_target_pairs={{2,4},{3,5},{4,2},{5,3},{10,12},{11,13},{12,10},{13,11},{18,20},{1... | collective-permute-start | bytes 3145736 | tf_op jit(solution)/shard_map/ppermute | solution.py:121
  65.2 0.0 collective-permute-done.12
  65.2 0.0 collective-permute-done.11
  65.2 2.2 %collective-permute-start.13 = (bf16[256,2048]{1,0:T(8,128)(2,1)}, bf16[256,2048]{1,0:T(8,128)(2,1)}, u32[]{:S(2)}, u32[]{:S(2)}) collective-permute-start(bf16[256,2048]{1,0:T(8,128)(2,1)} %pad_maximum_fusion.1), channel_id=1, source_target_pairs={{0,24},{1,25},{2,26},{3,27},{4,28},{5,29},{6,30},{7,31},{8,16},{9,... | collective-permute-start | bytes 3145736 | tf_op jit(solution)/shard_map/ppermute | solution.py:121
  67.3 1.0 collective-permute-start.16
  68.4 0.0 collective-permute-start.17
  68.4 1.7 %pad_maximum_fusion = bf16[768,2048]{1,0:T(8,128)(2,1)S(1)} fusion(bf16[256,2048]{1,0:T(8,128)(2,1)} %collective-permute-done.12, bf16[256,2048]{1,0:T(8,128)(2,1)} %collective-permute-done.11, bf16[128,2048]{1,0:T(8,128)(2,1)S(1)} %collective-permute-done.10, bf16[128,2048]{1,0:T(8,128)(2,1)S(1)} %get-tuple-element.45), kind=kLoop, calls=%fused_computation | loop fusion | flops 12582912 | bytes 6291456 | tf_op jit(solution)/shard_map/concatenate | solution.py:169
  70.1 18.3 %collective-permute-done.6 = bf16[128,4096]{1,0:T(8,128)(2,1)} collective-permute-done((bf16[128,4096]{1,0:T(8,128)(2,1)}, bf16[128,4096]{1,0:T(8,128)(2,1)}, u32[]{:S(2)}, u32[]{:S(2)}) %collective-permute-start.6) | collective-permute-done | bytes 1048608 | tf_op jit(solution)/shard_map/ppermute | solution.py:121
  88.4 0.0 collective-permute-done.5
  88.4 1.0 collective-permute-done.13
  89.4 1.3 fusion
  90.7 1.3 collective-permute-start.14
  92.0 1.4 broadcast_select_fusion.refs_2_
  93.3 0.0 copy-start
  93.4 2.7 %collective-permute-start.18 = (bf16[128,4096]{1,0:T(8,128)(2,1)S(1)}, bf16[128,4096]{1,0:T(8,128)(2,1)S(1)}, u32[]{:S(2)}, u32[]{:S(2)}) collective-permute-start(bf16[128,4096]{1,0:T(8,128)(2,1)S(1)} %broadcast_select_fusion.refs_2_), channel_id=1, source_target_pairs={{0,1},{1,0},{2,3},{3,2},{4,5},{5,4},{6,7},{7,6},{8,9},{9,8},{10,11... | collective-permute-start | bytes 3145736 | tf_op jit(solution)/shard_map/ppermute | solution.py:121
  96.0 0.4 constant_dynamic-update-slice_fusion.9
  96.4 1.3 constant_dynamic-update-slice_fusion.8.col
  97.8 8.6 %collective-permute-done.14 = bf16[128,2048]{1,0:T(8,128)(2,1)S(1)} collective-permute-done((bf16[128,2048]{1,0:T(8,128)(2,1)S(1)}, bf16[128,2048]{1,0:T(8,128)(2,1)S(1)}, u32[]{:S(2)}, u32[]{:S(2)}) %collective-permute-start.14) | collective-permute-done | bytes 524320 | tf_op jit(solution)/shard_map/ppermute | solution.py:121
  106.4 1.1 slice_select_fusion.refs_3_
  107.5 2.7 %collective-permute-start.19 = (bf16[128,2048]{1,0:T(8,128)(2,1)S(1)}, bf16[128,2048]{1,0:T(8,128)(2,1)S(1)}, u32[]{:S(2)}, u32[]{:S(2)}) collective-permute-start(bf16[128,2048]{1,0:T(8,128)(2,1)S(1)} %slice_select_fusion.refs_3_), channel_id=1, source_target_pairs={{0,1},{1,0},{2,3},{3,2},{4,5},{5,4},{6,7},{7,6},{8,9},{9,8},{10,11... | collective-permute-start | bytes 1572872 | tf_op jit(solution)/shard_map/ppermute | solution.py:121
  110.2 1.3 collective-permute-start.15
  111.5 0.0 collective-permute-done.16.refs_4_
  111.5 0.0 collective-permute-done.17.refs_5_
  111.5 0.2 collective-permute-done.19.refs_7_
  111.7 0.0 collective-permute-done.18.refs_6_
  111.7 0.0 copy-done
  111.7 11.9 %product.2.refs_8_ = f32[4096,2048]{1,0:T(8,128)} custom-call(bf16[1024,2048]{1,0:T(8,128)(2,1)S(1)} %constant_dynamic-update-slice_fusion.8.col, f32[1,16384]{1,0:T(1,128)S(1)} %bitcast.1, bf16[128,4096]{1,0:T(8,128)(2,1)S(1)} %constant_dynamic-update-slice_fusion.refs_0_, bf16[128,4096]{1,0:T(8,128)(2,1)S(1)} %collective-permute-done.3.refs_1_, ...), custom_call_target="tpu_custom_call" | custom-call | tf_op jit(solution)/shard_map/product/pallas_call | solution.py:79
  123.7 1.9 %collective-permute-done.15 = bf16[128,2048]{1,0:T(8,128)(2,1)S(1)} collective-permute-done((bf16[128,2048]{1,0:T(8,128)(2,1)S(1)}, bf16[128,2048]{1,0:T(8,128)(2,1)S(1)}, u32[]{:S(2)}, u32[]{:S(2)}) %collective-permute-start.15) | collective-permute-done | bytes 524320 | tf_op jit(solution)/shard_map/ppermute | solution.py:121
  125.6 1.1 slice_select_fusion.1.refs_3_
  126.7 0.9 collective-permute-start.20
  127.6 1.5 %collective-permute-done.20.refs_7_ = bf16[128,2048]{1,0:T(8,128)(2,1)S(1)} collective-permute-done((bf16[128,2048]{1,0:T(8,128)(2,1)S(1)}, bf16[128,2048]{1,0:T(8,128)(2,1)S(1)}, u32[]{:S(2)}, u32[]{:S(2)}) %collective-permute-start.20) | collective-permute-done | bytes 524320 | tf_op jit(solution)/shard_map/ppermute | solution.py:121
  129.1 13.7 %product.3 = f32[4096,2048]{1,0:T(8,128)} custom-call(bf16[1024,2048]{1,0:T(8,128)(2,1)S(1)} %constant_dynamic-update-slice_fusion.8.col, f32[1,16384]{1,0:T(1,128)S(1)} %bitcast.2, bf16[128,4096]{1,0:T(8,128)(2,1)S(1)} %constant_dynamic-update-slice_fusion.refs_0_, ...), custom_call_target="tpu_custom_call", output_to_operand_aliasing={{}: (10, {})} | custom-call | tf_op jit(solution)/shard_map/product/pallas_call | solution.py:79
  (5 shorter events, 0.1 us)
Async XLA Ops:
  2.8 8.8 %collective-permute-start = (bf16[32,4096]{1,0:T(8,128)(2,1)}, bf16[32,4096]{1,0:T(8,128)(2,1)S(1)}, u32[]{:S(2)}, u32[]{:S(2)}) collective-permute-start(bf16[32,4096]{1,0:T(8,128)(2,1)} %get-tuple-element.25), channel_id=1, source_target_pairs={{0,8},{1,9},{2,10},{3,11},{4,12},{5,13},{6,14},{7,15},{8,0},{9,1},... | collective-permute-start | bytes 786440 | tf_op jit(solution)/shard_map/ppermute | solution.py:121
  4.8 26.1 %collective-permute-start.1 = (bf16[32,4096]{1,0:T(8,128)(2,1)}, bf16[32,4096]{1,0:T(8,128)(2,1)}, u32[]{:S(2)}, u32[]{:S(2)}) collective-permute-start(bf16[32,4096]{1,0:T(8,128)(2,1)} %get-tuple-element.26), channel_id=1, source_target_pairs={{0,16},{1,17},{2,18},{3,19},{4,20},{5,21},{6,22},{7,23},{8,24},{9,... | collective-permute-start | bytes 786440 | tf_op jit(solution)/shard_map/ppermute | solution.py:121
  6.1 25.9 %collective-permute-start.2 = (bf16[32,4096]{1,0:T(8,128)(2,1)}, bf16[32,4096]{1,0:T(8,128)(2,1)S(1)}, u32[]{:S(2)}, u32[]{:S(2)}) collective-permute-start(bf16[32,4096]{1,0:T(8,128)(2,1)} %get-tuple-element.27), channel_id=1, source_target_pairs={{0,24},{1,25},{2,26},{3,27},{4,28},{5,29},{6,30},{7,31},{8,16},{9,... | collective-permute-start | bytes 786440 | tf_op jit(solution)/shard_map/ppermute | solution.py:121
  6.1 22.8 %collective-permute-start.8 = (bf16[32,4096]{1,0:T(8,128)(2,1)}, bf16[32,4096]{1,0:T(8,128)(2,1)S(1)}, u32[]{:S(2)}, u32[]{:S(2)}) collective-permute-start(bf16[32,4096]{1,0:T(8,128)(2,1)} %get-tuple-element.33), channel_id=1, source_target_pairs={{0,4},{1,5},{2,6},{3,7},{4,0},{5,1},{6,2},{7,3},{8,12},{9,13},{10,... | collective-permute-start | bytes 786440 | tf_op jit(solution)/shard_map/ppermute | solution.py:121
  8.6 20.3 %collective-permute-start.9 = (bf16[32,4096]{1,0:T(8,128)(2,1)}, bf16[32,4096]{1,0:T(8,128)(2,1)S(1)}, u32[]{:S(2)}, u32[]{:S(2)}) collective-permute-start(bf16[32,4096]{1,0:T(8,128)(2,1)} %get-tuple-element.34), channel_id=1, source_target_pairs={{0,6},{1,7},{2,4},{3,5},{4,2},{5,3},{6,0},{7,1},{8,14},{9,15},{10,... | collective-permute-start | bytes 786440 | tf_op jit(solution)/shard_map/ppermute | solution.py:121
  11.6 17.2 %collective-permute-start.7 = (bf16[32,4096]{1,0:T(8,128)(2,1)}, bf16[32,4096]{1,0:T(8,128)(2,1)S(1)}, u32[]{:S(2)}, u32[]{:S(2)}) collective-permute-start(bf16[32,4096]{1,0:T(8,128)(2,1)} %get-tuple-element.32), channel_id=1, source_target_pairs={{0,2},{1,3},{2,0},{3,1},{4,6},{5,7},{6,4},{7,5},{8,10},{9,11},{10,... | collective-permute-start | bytes 786440 | tf_op jit(solution)/shard_map/ppermute | solution.py:121
  29.0 9.8 %collective-permute-start.10 = (bf16[128,2048]{1,0:T(8,128)(2,1)S(1)}, bf16[128,2048]{1,0:T(8,128)(2,1)S(1)}, u32[]{:S(2)}, u32[]{:S(2)}) collective-permute-start(bf16[128,2048]{1,0:T(8,128)(2,1)S(1)} %get-tuple-element.46), channel_id=1, source_target_pairs={{0,1},{1,0},{2,3},{3,2},{4,5},{5,4},{6,7},{7,6},{8,9},{9,8},{10,11... | collective-permute-start | bytes 1572872 | tf_op jit(solution)/shard_map/ppermute | solution.py:121
  32.0 10.3 %collective-permute-start.4 = (bf16[128,4096]{1,0:T(8,128)(2,1)S(1)}, bf16[128,4096]{1,0:T(8,128)(2,1)}, u32[]{:S(2)}, u32[]{:S(2)}) collective-permute-start(bf16[128,4096]{1,0:T(8,128)(2,1)S(1)} %constant_dynamic-update-slice_fusion.refs_0_), channel_id=1, source_target_pairs={{2,4},{3,5},{4,2},{5,3},{10,12},{11,13},{12,10},{13,11},{18,20},{1... | collective-permute-start | bytes 3145736 | tf_op jit(solution)/shard_map/ppermute | solution.py:121
  33.6 28.6 %collective-permute-start.3 = (bf16[128,4096]{1,0:T(8,128)(2,1)S(1)}, bf16[128,4096]{1,0:T(8,128)(2,1)S(1)}, u32[]{:S(2)}, u32[]{:S(2)}) collective-permute-start(bf16[128,4096]{1,0:T(8,128)(2,1)S(1)} %constant_dynamic-update-slice_fusion.refs_0_), channel_id=1, source_target_pairs={{0,2},{1,3},{2,0},{3,1},{4,6},{5,7},{6,4},{7,5},{8,10},{9,11},{10,... | collective-permute-start | bytes 3145736 | tf_op jit(solution)/shard_map/ppermute | solution.py:121
  39.8 25.3 %collective-permute-start.12 = (bf16[256,2048]{1,0:T(8,128)(2,1)}, bf16[256,2048]{1,0:T(8,128)(2,1)}, u32[]{:S(2)}, u32[]{:S(2)}) collective-permute-start(bf16[256,2048]{1,0:T(8,128)(2,1)} %pad_maximum_fusion.1), channel_id=1, source_target_pairs={{0,16},{1,17},{2,18},{3,19},{4,20},{5,21},{6,22},{7,23},{8,24},{9,... | collective-permute-start | bytes 3145736 | tf_op jit(solution)/shard_map/ppermute | solution.py:121
  41.1 24.1 %collective-permute-start.11 = (bf16[256,2048]{1,0:T(8,128)(2,1)}, bf16[256,2048]{1,0:T(8,128)(2,1)}, u32[]{:S(2)}, u32[]{:S(2)}) collective-permute-start(bf16[256,2048]{1,0:T(8,128)(2,1)} %pad_maximum_fusion.1), channel_id=1, source_target_pairs={{0,8},{1,9},{2,10},{3,11},{4,12},{5,13},{6,14},{7,15},{8,0},{9,1},... | collective-permute-start | bytes 3145736 | tf_op jit(solution)/shard_map/ppermute | solution.py:121
  62.2 26.2 %collective-permute-start.6 = (bf16[128,4096]{1,0:T(8,128)(2,1)}, bf16[128,4096]{1,0:T(8,128)(2,1)}, u32[]{:S(2)}, u32[]{:S(2)}) collective-permute-start(bf16[128,4096]{1,0:T(8,128)(2,1)} %collective-permute-done.4), channel_id=1, source_target_pairs={{2,0},{3,1},{4,6},{5,7},{10,8},{11,9},{12,14},{13,15},{18,16},{19,... | collective-permute-start | bytes 3145736 | tf_op jit(solution)/shard_map/ppermute | solution.py:121
  63.5 24.9 %collective-permute-start.5 = (bf16[128,4096]{1,0:T(8,128)(2,1)S(1)}, bf16[128,4096]{1,0:T(8,128)(2,1)}, u32[]{:S(2)}, u32[]{:S(2)}) collective-permute-start(bf16[128,4096]{1,0:T(8,128)(2,1)S(1)} %collective-permute-done.3.refs_1_), channel_id=1, source_target_pairs={{2,4},{3,5},{4,2},{5,3},{10,12},{11,13},{12,10},{13,11},{18,20},{1... | collective-permute-start | bytes 3145736 | tf_op jit(solution)/shard_map/ppermute | solution.py:121
  65.2 24.2 %collective-permute-start.13 = (bf16[256,2048]{1,0:T(8,128)(2,1)}, bf16[256,2048]{1,0:T(8,128)(2,1)}, u32[]{:S(2)}, u32[]{:S(2)}) collective-permute-start(bf16[256,2048]{1,0:T(8,128)(2,1)} %pad_maximum_fusion.1), channel_id=1, source_target_pairs={{0,24},{1,25},{2,26},{3,27},{4,28},{5,29},{6,30},{7,31},{8,16},{9,... | collective-permute-start | bytes 3145736 | tf_op jit(solution)/shard_map/ppermute | solution.py:121
  67.3 44.1 %collective-permute-start.16 = (bf16[128,4096]{1,0:T(8,128)(2,1)S(1)}, bf16[128,4096]{1,0:T(8,128)(2,1)S(1)}, u32[]{:S(2)}, u32[]{:S(2)}) collective-permute-start(bf16[128,4096]{1,0:T(8,128)(2,1)S(1)} %constant_dynamic-update-slice_fusion.refs_0_), channel_id=1, source_target_pairs={{0,1},{1,0},{2,3},{3,2},{4,5},{5,4},{6,7},{7,6},{8,9},{9,8},{10,11... | collective-permute-start | bytes 3145736 | tf_op jit(solution)/shard_map/ppermute | solution.py:121
  68.4 43.1 %collective-permute-start.17 = (bf16[128,4096]{1,0:T(8,128)(2,1)S(1)}, bf16[128,4096]{1,0:T(8,128)(2,1)S(1)}, u32[]{:S(2)}, u32[]{:S(2)}) collective-permute-start(bf16[128,4096]{1,0:T(8,128)(2,1)S(1)} %collective-permute-done.3.refs_1_), channel_id=1, source_target_pairs={{0,1},{1,0},{2,3},{3,2},{4,5},{5,4},{6,7},{7,6},{8,9},{9,8},{10,11... | collective-permute-start | bytes 3145736 | tf_op jit(solution)/shard_map/ppermute | solution.py:121
  90.7 15.7 %collective-permute-start.14 = (bf16[128,2048]{1,0:T(8,128)(2,1)S(1)}, bf16[128,2048]{1,0:T(8,128)(2,1)S(1)}, u32[]{:S(2)}, u32[]{:S(2)}) collective-permute-start(bf16[128,2048]{1,0:T(8,128)(2,1)S(1)} %get-tuple-element.43), channel_id=1, source_target_pairs={{2,0},{3,1},{4,6},{5,7},{10,8},{11,9},{12,14},{13,15},{18,16},{19,... | collective-permute-start | bytes 1572872 | tf_op jit(solution)/shard_map/ppermute | solution.py:121
  93.3 18.4 %copy-start = (f32[16384]{0:T(1024)S(1)}, f32[16384]{0:T(1024)}, u32[]{:S(2)}) copy-start(f32[16384]{0:T(1024)} %param.5) | copy-start | bytes 196612
  93.4 18.4 %collective-permute-start.18 = (bf16[128,4096]{1,0:T(8,128)(2,1)S(1)}, bf16[128,4096]{1,0:T(8,128)(2,1)S(1)}, u32[]{:S(2)}, u32[]{:S(2)}) collective-permute-start(bf16[128,4096]{1,0:T(8,128)(2,1)S(1)} %broadcast_select_fusion.refs_2_), channel_id=1, source_target_pairs={{0,1},{1,0},{2,3},{3,2},{4,5},{5,4},{6,7},{7,6},{8,9},{9,8},{10,11... | collective-permute-start | bytes 3145736 | tf_op jit(solution)/shard_map/ppermute | solution.py:121
  107.5 4.2 %collective-permute-start.19 = (bf16[128,2048]{1,0:T(8,128)(2,1)S(1)}, bf16[128,2048]{1,0:T(8,128)(2,1)S(1)}, u32[]{:S(2)}, u32[]{:S(2)}) collective-permute-start(bf16[128,2048]{1,0:T(8,128)(2,1)S(1)} %slice_select_fusion.refs_3_), channel_id=1, source_target_pairs={{0,1},{1,0},{2,3},{3,2},{4,5},{5,4},{6,7},{7,6},{8,9},{9,8},{10,11... | collective-permute-start | bytes 1572872 | tf_op jit(solution)/shard_map/ppermute | solution.py:121
  110.2 15.4 %collective-permute-start.15 = (bf16[128,2048]{1,0:T(8,128)(2,1)S(1)}, bf16[128,2048]{1,0:T(8,128)(2,1)S(1)}, u32[]{:S(2)}, u32[]{:S(2)}) collective-permute-start(bf16[128,2048]{1,0:T(8,128)(2,1)S(1)} %get-tuple-element.40), channel_id=1, source_target_pairs={{2,0},{3,1},{4,6},{5,7},{10,8},{11,9},{12,14},{13,15},{18,16},{19,... | collective-permute-start | bytes 1572872 | tf_op jit(solution)/shard_map/ppermute | solution.py:121
  126.7 2.4 %collective-permute-start.20 = (bf16[128,2048]{1,0:T(8,128)(2,1)S(1)}, bf16[128,2048]{1,0:T(8,128)(2,1)S(1)}, u32[]{:S(2)}, u32[]{:S(2)}) collective-permute-start(bf16[128,2048]{1,0:T(8,128)(2,1)S(1)} %slice_select_fusion.1.refs_3_), channel_id=1, source_target_pairs={{0,1},{1,0},{2,3},{3,2},{4,5},{5,4},{6,7},{7,6},{8,9},{9,8},{10,11... | collective-permute-start | bytes 1572872 | tf_op jit(solution)/shard_map/ppermute | solution.py:121

commit v3 on v2

--- a/solution.py
+++ b/solution.py
@@ -47,14 +47,21 @@
     )(mask, slab)
 
 
-def product_kernel(count, lines, total, first, col, damp, *refs):
-    parts = refs[:count]
+def product_kernel(picks, lines, total, first, col, damp, *refs):
     out = refs[-1]
     step = pl.program_id(0)
     rows, cols = out.shape
-    group = parts[0].shape[0] // lines
+    plane = lax.axis_index("col") // CORES
+    inner = (plane == 1) | (plane == 2)
+    slots = []
+    for pick in picks:
+        value = refs[pick[0]][...]
+        if len(pick) == 2:
+            value = jnp.where(inner, value, refs[pick[1]][...])
+        slots.append(value)
+    group = slots[0].shape[0] // lines
     left = jnp.concatenate(
-        [part[m * group : (m + 1) * group, :] for m in range(lines) for part in parts], axis=0
+        [slot[m * group : (m + 1) * group, :] for m in range(lines) for slot in slots], axis=0
     )
     out[...] = lax.dot_general(
         left, col[...], (((0,), (0,)), ((), ())), preferred_element_type=jnp.float32
@@ -70,14 +77,18 @@
         out[...] += jnp.where(row_ids == col_ids, mine, 0.0)
 
 
-def product(parts, col, damp, lines, total, first, width, block):
+def product(slots, col, damp, lines, total, first, width, block):
+    parts, picks = [], []
+    for slot in slots:
+        picks.append(tuple(range(len(parts), len(parts) + len(slot))))
+        parts.extend(slot)
     depth = parts[0].shape[0]
     rows = math.gcd(BLOCK_ROWS, width, first)
     steps = width // rows
     held, cols = col.shape
     count = len(parts)
     return pl.pallas_call(
-        functools.partial(product_kernel, count, lines, total, first),
+        functools.partial(product_kernel, picks, lines, total, first),
         out_shape=jax.ShapeDtypeStruct((total, cols), jnp.float32),
         grid=(steps,),
         in_specs=[
@@ -138,10 +149,10 @@
     picked = pick_panels(slab, block_mask, lines, planes)
     by_line, by_plane = picked[:lines], picked[lines:]
 
-    row_parts = [by_line[0]] + [across_lines(by_line[m], m) for m in range(1, lines)]
-    col_parts = [by_plane[0]]
-    for k in range(1, planes):
-        col_parts.append(across_planes(after(by_plane[k], row_parts[1]) if k == 1 else by_plane[k], k))
+    col_parts = [by_plane[0]] + [across_planes(by_plane[k], k) for k in range(planes - 1, 0, -1)][::-1]
+    row_parts = [by_line[0]]
+    for m in range(1, lines):
+        row_parts.append(across_lines(after(by_line[m], *row_parts[1:2]) if m == 3 else by_line[m], m))
     mine = jnp.concatenate(col_parts, axis=0)
     keep = lax.dynamic_slice_in_dim(mine, core * half, half, 1)
     give = lax.dynamic_slice_in_dim(mine, (1 - core) * half, half, 1)
@@ -165,35 +176,33 @@
         near, mid = lax.optimization_barrier((near, mid))
         far_in = swap_inner(near)
         far_out = push_out(mid)
-        third = across_lines(after(mine, near, mid, one, two), 3)
+        third = across_lines(mine, 3)
+        first_own = after(cut(own)[0], near, mid)
+        direct = send(first_own, lambda r, q, c: (r, q ^ 3, c) if q in (0, 3) else None)
         held = jnp.concatenate([mine, one, two], axis=0)
-        far_in, far_out, third, held = lax.optimization_barrier((far_in, far_out, third, held))
         col_panel = jnp.concatenate([held, third], axis=0)
-        last = []
-        for piece in cut(far_in):
-            last.append(push_out(after(piece, *last, *([col_panel] if last else []))))
+        far_in, far_out, col_panel, direct = lax.optimization_barrier(
+            (far_in, far_out, col_panel, direct)
+        )
+        last = [direct, push_out(cut(far_in)[1])]
         far = jnp.where(inner, far_in, far_out)
-        across = [across_cores(p) for p in (own, near, far)]
-        split = list(zip(cut(mid), last))
-        full = [own, near, far] + across
+        slots = [[p] for p in (own, near, far, mid)]
     else:
         col_lines = [mine] + [across_lines(mine, m) for m in range(1, lines)]
-        full = [own] + [across_planes(own, k) for k in range(1, planes)]
-        full += [across_cores(p) for p in full]
-        split = [None] * len(CHUNKS)
         col_panel = jnp.concatenate(col_lines, axis=0)
-
+        slots = [[own]] + [[across_planes(own, k)] for k in range(1, planes)]
+        last = [None] * len(CHUNKS)
+
+    sides = [[across_cores(p) for p in slot] for slot in slots]
     out = None
-    for first, end, pair in zip(cuts, cuts[1:], split):
-        parts = full
-        if pair is not None:
-            middle, outer = pair
+    for first, end, outer in zip(cuts, cuts[1:], last):
+        ours, theirs = slots, sides
+        if outer is not None:
             if out is not None:
                 outer, out = lax.optimization_barrier((outer, out))
-            part = jnp.where(inner, middle, outer)
-            at = len(full) // 2
-            parts = full[:at] + [part] + full[at:] + [across_cores(part)]
-        out = product(parts, col_panel, damping[None, :], lines, panel, first, end - first, out)
+            ours = slots[:3] + [slots[3] + [outer]]
+            theirs = sides[:3] + [sides[3] + [across_cores(outer)]]
+        out = product(ours + theirs, col_panel, damping[None, :], lines, panel, first, end - first, out)
     return out
 
 

time: 143 us -> 137 us (0.958)
  waiting for transfers between devices: 68 us -> 43.3 us
  starting transfers between devices: 33.8 us -> 50 us
  local copies, waits for them, and re-layouts: 6.14 us -> 12 us
  other arithmetic: 6.27 us -> 2.52 us
    ppermute x21 -> x22, waiting for transfers between devices: 68 us -> 43.3 us  [send(): return lax.ppermute(value, AXES, flat)]
    ppermute x21 -> x22, starting transfers between devices: 33.8 us -> 50 us  [send(): return lax.ppermute(value, AXES, flat)]
    unnamed x9 -> x15, local copies, waits for them, and re-layouts: 3.37 us -> 8.59 us
    select_n x2 -> x0, other arithmetic: 2.2 us -> none  [shards(): part = jnp.where(inner, middle, outer)]
    concatenate x1 -> x0, other arithmetic: 1.68 us -> none  [shards(): held = jnp.concatenate([mine, one, two], axis=0)]
  transfers between devices with their start and end apart: 21 -> 22, of which waited for: 8 -> 9; matrix products, arithmetic and copies ran while one was open for 8% -> 11% of each run, Pallas kernels for 8% -> 9%
where the time goes in v3:
time: 137 us
  starting transfers between devices  50 us (36%)
  waiting for transfers between devices  43.3 us (32%)
  Pallas kernels  28.8 us (21%)
  local copies, waits for them, and re-layouts  12 us (9%)
  other arithmetic  2.52 us (2%)
    ppermute x22, starting transfers between devices, send(): return lax.ppermute(value, AXES, flat)  50 us
    ppermute x22, waiting for transfers between devices, send(): return lax.ppermute(value, AXES, flat)  43.3 us
    pallas_call x2, Pallas kernels, product(): pl.pallas_call(functools.partial(product_kernel, picks, lines, total, fir...  26 us
    unnamed x15, local copies, waits for them, and re-layouts  8.59 us
    pallas_call x1, Pallas kernels, pick_panels(): pl.pallas_call(functools.partial(pick_kernel, lines), out_shape=[jax.Shap...  2.78 us
  transfers between devices with their start and end apart: 22, of which 9 were waited for; matrix products, arithmetic and copies ran while one was open for 11% of the time, Pallas kernels for 9%

profile of v3, /device:TPU:1, one launch (start us, length us, event | category | flops | bytes accessed | tf_op | source)
XLA Modules:
  0.0 136.8 jit_solution(11349691407968192013)
XLA Ops:
  0.0 2.8 %pick_panels.1 = (bf16[32,4096]{1,0:T(8,128)(2,1)}, bf16[32,4096]{1,0:T(8,128)(2,1)}, bf16[32,4096]{1,0:T(8,128)(2,1)}, bf16[32,4096]{1,0:T(8,128)(2,1)}, bf16[3...) custom-call(s32[1,16]{1,0:T(1,128)} %mask.1, ...), custom_call_target="tpu_custom_call" | custom-call | tf_op jit(solution)/shard_map/pick_panels/pallas_call | solution.py:38
  2.8 2.0 %collective-permute-start = (bf16[32,4096]{1,0:T(8,128)(2,1)}, bf16[32,4096]{1,0:T(8,128)(2,1)S(1)}, u32[]{:S(2)}, u32[]{:S(2)}) collective-permute-start(bf16[32,4096]{1,0:T(8,128)(2,1)} %get-tuple-element.24), channel_id=1, source_target_pairs={{0,8},{1,9},{2,10},{3,11},{4,12},{5,13},{6,14},{7,15},{8,0},{9,1},... | collective-permute-start | bytes 786440 | tf_op jit(solution)/shard_map/ppermute | solution.py:132
  4.8 1.2 collective-permute-start.1
  6.1 1.3 collective-permute-start.7
  7.4 2.3 %collective-permute-start.8 = (bf16[32,4096]{1,0:T(8,128)(2,1)}, bf16[32,4096]{1,0:T(8,128)(2,1)S(1)}, u32[]{:S(2)}, u32[]{:S(2)}) collective-permute-start(bf16[32,4096]{1,0:T(8,128)(2,1)} %get-tuple-element.32), channel_id=1, source_target_pairs={{0,4},{1,5},{2,6},{3,7},{4,0},{5,1},{6,2},{7,3},{8,12},{9,13},{10,... | collective-permute-start | bytes 786440 | tf_op jit(solution)/shard_map/ppermute | solution.py:132
  9.7 0.0 collective-permute-start.9
  9.7 1.1 constant_dynamic-update-slice_fusion.3
  10.7 0.3 collective-permute-done
  11.1 2.1 %collective-permute-start.2 = (bf16[32,4096]{1,0:T(8,128)(2,1)}, bf16[32,4096]{1,0:T(8,128)(2,1)S(1)}, u32[]{:S(2)}, u32[]{:S(2)}) collective-permute-start(bf16[32,4096]{1,0:T(8,128)(2,1)} %get-tuple-element.27), channel_id=1, source_target_pairs={{0,24},{1,25},{2,26},{3,27},{4,28},{5,29},{6,30},{7,31},{8,16},{9,... | collective-permute-start | bytes 786440 | tf_op jit(solution)/shard_map/ppermute | solution.py:132
  13.2 3.8 %collective-permute-done.7 = bf16[32,4096]{1,0:T(8,128)(2,1)S(1)} collective-permute-done((bf16[32,4096]{1,0:T(8,128)(2,1)}, bf16[32,4096]{1,0:T(8,128)(2,1)S(1)}, u32[]{:S(2)}, u32[]{:S(2)}) %collective-permute-start.7) | collective-permute-done | bytes 262176 | tf_op jit(solution)/shard_map/ppermute | solution.py:132
  17.0 0.7 collective-permute-done.8
  17.7 8.4 %collective-permute-done.9 = bf16[32,4096]{1,0:T(8,128)(2,1)S(1)} collective-permute-done((bf16[32,4096]{1,0:T(8,128)(2,1)}, bf16[32,4096]{1,0:T(8,128)(2,1)S(1)}, u32[]{:S(2)}, u32[]{:S(2)}) %collective-permute-start.9) | collective-permute-done | bytes 262176 | tf_op jit(solution)/shard_map/ppermute | solution.py:132
  26.2 0.9 constant_dynamic-update-slice_fusion.12
  27.1 4.4 %collective-permute-start.10 = (bf16[128,2048]{1,0:T(8,128)(2,1)S(1)}, bf16[128,2048]{1,0:T(8,128)(2,1)S(1)}, u32[]{:S(2)}, u32[]{:S(2)}) collective-permute-start(bf16[128,2048]{1,0:T(8,128)(2,1)S(1)} %get-tuple-element.43), channel_id=1, source_target_pairs={{0,1},{1,0},{2,3},{3,2},{4,5},{5,4},{6,7},{7,6},{8,9},{9,8},{10,11... | collective-permute-start | bytes 1572872 | tf_op jit(solution)/shard_map/ppermute | solution.py:132
  31.5 0.0 collective-permute-done.1
  31.5 0.0 collective-permute-done.2
  31.6 0.7 collective-permute-start.4
  32.3 6.4 %collective-permute-start.3 = (bf16[128,4096]{1,0:T(8,128)(2,1)S(1)}, bf16[128,4096]{1,0:T(8,128)(2,1)S(1)}, u32[]{:S(2)}, u32[]{:S(2)}) collective-permute-start(bf16[128,4096]{1,0:T(8,128)(2,1)S(1)} %constant_dynamic-update-slice_fusion.refs_0_), channel_id=1, source_target_pairs={{0,2},{1,3},{2,0},{3,1},{4,6},{5,7},{6,4},{7,5},{8,10},{9,11},{10,... | collective-permute-start | bytes 3145736 | tf_op jit(solution)/shard_map/ppermute | solution.py:132
  38.7 0.0 collective-permute-done.10
  38.7 0.0 copy-start.2
  38.7 1.2 pad_maximum_fusion
  39.9 0.3 collective-permute-start.11
  40.2 0.2 collective-permute-start.12
  40.4 2.2 %collective-permute-start.13 = (bf16[256,2048]{1,0:T(8,128)(2,1)}, bf16[256,2048]{1,0:T(8,128)(2,1)}, u32[]{:S(2)}, u32[]{:S(2)}) collective-permute-start(bf16[256,2048]{1,0:T(8,128)(2,1)} %pad_maximum_fusion), channel_id=1, source_target_pairs={{0,24},{1,25},{2,26},{3,27},{4,28},{5,29},{6,30},{7,31},{8,16},{9,... | collective-permute-start | bytes 3145736 | tf_op jit(solution)/shard_map/ppermute | solution.py:132
  42.5 0.0 collective-permute-done.4.refs_3_
  42.6 19.6 %collective-permute-done.3.refs_1_ = bf16[128,4096]{1,0:T(8,128)(2,1)S(1)} collective-permute-done((bf16[128,4096]{1,0:T(8,128)(2,1)S(1)}, bf16[128,4096]{1,0:T(8,128)(2,1)S(1)}, u32[]{:S(2)}, u32[]{:S(2)}) %collective-permute-start.3) | collective-permute-done | bytes 1048608 | tf_op jit(solution)/shard_map/ppermute | solution.py:132
  62.1 0.0 copy-done.2
  62.2 1.6 %collective-permute-start.5 = (bf16[128,4096]{1,0:T(8,128)(2,1)S(1)}, bf16[128,4096]{1,0:T(8,128)(2,1)}, u32[]{:S(2)}, u32[]{:S(2)}) collective-permute-start(bf16[128,4096]{1,0:T(8,128)(2,1)S(1)} %collective-permute-done.3.refs_1_), channel_id=1, source_target_pairs={{2,4},{3,5},{4,2},{5,3},{10,12},{11,13},{12,10},{13,11},{18,20},{1... | collective-permute-start | bytes 3145736 | tf_op jit(solution)/shard_map/ppermute | solution.py:132
  63.8 1.3 collective-permute-start.6
  65.1 1.9 %constant_dynamic-update-slice_fusion.11 = bf16[1024,2048]{1,0:T(8,128)(2,1)} fusion(bf16[1024,2048]{1,0:T(8,128)(2,1)} %get-tuple-element.41, bf16[128,2048]{1,0:T(8,128)(2,1)} %copy-done.2), kind=kLoop, calls=%fused_computation.13 | loop fusion | bytes 1048576
  67.0 0.0 collective-permute-done.11
  67.0 3.0 %collective-permute-start.14 = (bf16[128,2048]{1,0:T(8,128)(2,1)S(1)}, bf16[128,2048]{1,0:T(8,128)(2,1)S(1)}, u32[]{:S(2)}, u32[]{:S(2)}) collective-permute-start(bf16[128,2048]{1,0:T(8,128)(2,1)S(1)} %slice.8), channel_id=1, source_target_pairs={{0,6},{1,7},{6,0},{7,1},{8,14},{9,15},{14,8},{15,9},{16,22},{17,23... | collective-permute-start | bytes 1572872 | tf_op jit(solution)/shard_map/ppermute | solution.py:132
  70.0 2.3 %constant_dynamic-update-slice_fusion.10 = bf16[1024,2048]{1,0:T(8,128)(2,1)} fusion(bf16[1024,2048]{1,0:T(8,128)(2,1)} %constant_dynamic-update-slice_fusion.11, bf16[256,2048]{1,0:T(8,128)(2,1)} %collective-permute-done.11), kind=kLoop, calls=%fused_computation.12 | loop fusion | bytes 2097152
  72.3 0.0 copy-start.1
  72.3 0.0 collective-permute-done.12
  72.3 16.2 %collective-permute-start.16 = (bf16[128,4096]{1,0:T(8,128)(2,1)S(1)}, bf16[128,4096]{1,0:T(8,128)(2,1)S(1)}, u32[]{:S(2)}, u32[]{:S(2)}) collective-permute-start(bf16[128,4096]{1,0:T(8,128)(2,1)S(1)} %constant_dynamic-update-slice_fusion.refs_0_), channel_id=1, source_target_pairs={{0,1},{1,0},{2,3},{3,2},{4,5},{5,4},{6,7},{7,6},{8,9},{9,8},{10,11... | collective-permute-start | bytes 3145736 | tf_op jit(solution)/shard_map/ppermute | solution.py:132
  88.5 2.3 %constant_dynamic-update-slice_fusion.9 = bf16[1024,2048]{1,0:T(8,128)(2,1)} fusion(bf16[1024,2048]{1,0:T(8,128)(2,1)} %constant_dynamic-update-slice_fusion.10, bf16[256,2048]{1,0:T(8,128)(2,1)} %collective-permute-done.12), kind=kLoop, calls=%fused_computation.11 | loop fusion | bytes 2097152
  90.8 0.0 collective-permute-done.13
  90.8 0.0 collective-permute-start.17
  90.8 2.3 %constant_dynamic-update-slice_fusion.8.col = bf16[1024,2048]{1,0:T(8,128)(2,1)} fusion(bf16[1024,2048]{1,0:T(8,128)(2,1)} %constant_dynamic-update-slice_fusion.9, bf16[256,2048]{1,0:T(8,128)(2,1)} %collective-permute-done.13), kind=kLoop, calls=%fused_computation.10 | loop fusion | bytes 2097152 | tf_op jit(solution)/shard_map/concatenate | solution.py:183
  93.1 0.0 copy-start
  93.1 0.0 collective-permute-done.14.refs_4_
  93.1 0.5 collective-permute-start.19
  93.6 0.0 collective-permute-done.5
  93.6 7.4 %collective-permute-done.6 = bf16[128,4096]{1,0:T(8,128)(2,1)} collective-permute-done((bf16[128,4096]{1,0:T(8,128)(2,1)S(1)}, bf16[128,4096]{1,0:T(8,128)(2,1)}, u32[]{:S(2)}, u32[]{:S(2)}) %collective-permute-start.6) | collective-permute-done | bytes 1048608 | tf_op jit(solution)/shard_map/ppermute | solution.py:132
  101.0 1.3 broadcast_select_fusion.refs_2_
  102.3 1.6 %collective-permute-start.18 = (bf16[128,4096]{1,0:T(8,128)(2,1)S(1)}, bf16[128,4096]{1,0:T(8,128)(2,1)S(1)}, u32[]{:S(2)}, u32[]{:S(2)}) collective-permute-start(bf16[128,4096]{1,0:T(8,128)(2,1)S(1)} %broadcast_select_fusion.refs_2_), channel_id=1, source_target_pairs={{0,1},{1,0},{2,3},{3,2},{4,5},{5,4},{6,7},{7,6},{8,9},{9,8},{10,11... | collective-permute-start | bytes 3145736 | tf_op jit(solution)/shard_map/ppermute | solution.py:132
  104.0 0.1 collective-permute-start.20
  104.0 1.1 slice.7
  105.1 0.0 collective-permute-done.16.refs_5_
  105.1 1.3 collective-permute-start.15
  106.4 0.0 collective-permute-done.17.refs_6_
  106.4 0.0 collective-permute-done.19.refs_8_
  106.5 0.5 collective-permute-done.20.refs_9_
  107.0 0.0 collective-permute-done.18.refs_7_
  107.0 0.0 copy-done.1
  107.0 0.0 copy-done
  107.0 12.1 %product.2.refs_10_ = f32[4096,2048]{1,0:T(8,128)} custom-call(bf16[1024,2048]{1,0:T(8,128)(2,1)S(1)} %copy-done, f32[1,16384]{1,0:T(1,128)S(1)} %bitcast.1, bf16[128,4096]{1,0:T(8,128)(2,1)S(1)} %constant_dynamic-update-slice_fusion.refs_0_, bf16[128,4096]{1,0:T(8,128)(2,1)S(1)} %collective-permute-done.3.refs_1_, ...), custom_call_target="tpu_custom_call" | custom-call | tf_op jit(solution)/shard_map/product/pallas_call | solution.py:90
  119.1 1.0 collective-permute-done.15.refs_4_
  120.1 1.3 collective-permute-start.21
  121.4 1.5 %collective-permute-done.21.refs_9_ = bf16[128,2048]{1,0:T(8,128)(2,1)S(1)} collective-permute-done((bf16[128,2048]{1,0:T(8,128)(2,1)S(1)}, bf16[128,2048]{1,0:T(8,128)(2,1)S(1)}, u32[]{:S(2)}, u32[]{:S(2)}) %collective-permute-start.21) | collective-permute-done | bytes 524320 | tf_op jit(solution)/shard_map/ppermute | solution.py:132
  122.9 13.9 %product.3 = f32[4096,2048]{1,0:T(8,128)} custom-call(bf16[1024,2048]{1,0:T(8,128)(2,1)S(1)} %copy-done, f32[1,16384]{1,0:T(1,128)S(1)} %bitcast.2, bf16[128,4096]{1,0:T(8,128)(2,1)S(1)} %constant_dynamic-update-slice_fusion.refs_0_, bf16[128,4096]{1,0:T(8,128)(2,1)S(1)} %collective-permute-done.3.refs_1_, ...), custom_call_target="tpu_custom_call", output_to_operand_aliasing={{}: (12, {})} | custom-call | tf_op jit(solution)/shard_map/product/pallas_call | solution.py:90
  (7 shorter events, 0.1 us)
Async XLA Ops:
  2.8 8.3 %collective-permute-start = (bf16[32,4096]{1,0:T(8,128)(2,1)}, bf16[32,4096]{1,0:T(8,128)(2,1)S(1)}, u32[]{:S(2)}, u32[]{:S(2)}) collective-permute-start(bf16[32,4096]{1,0:T(8,128)(2,1)} %get-tuple-element.24), channel_id=1, source_target_pairs={{0,8},{1,9},{2,10},{3,11},{4,12},{5,13},{6,14},{7,15},{8,0},{9,1},... | collective-permute-start | bytes 786440 | tf_op jit(solution)/shard_map/ppermute | solution.py:132
  4.8 26.7 %collective-permute-start.1 = (bf16[32,4096]{1,0:T(8,128)(2,1)}, bf16[32,4096]{1,0:T(8,128)(2,1)S(1)}, u32[]{:S(2)}, u32[]{:S(2)}) collective-permute-start(bf16[32,4096]{1,0:T(8,128)(2,1)} %get-tuple-element.25), channel_id=1, source_target_pairs={{0,16},{1,17},{2,18},{3,19},{4,20},{5,21},{6,22},{7,23},{8,24},{9,... | collective-permute-start | bytes 786440 | tf_op jit(solution)/shard_map/ppermute | solution.py:132
  6.1 10.9 %collective-permute-start.7 = (bf16[32,4096]{1,0:T(8,128)(2,1)}, bf16[32,4096]{1,0:T(8,128)(2,1)S(1)}, u32[]{:S(2)}, u32[]{:S(2)}) collective-permute-start(bf16[32,4096]{1,0:T(8,128)(2,1)} %get-tuple-element.31), channel_id=1, source_target_pairs={{0,2},{1,3},{2,0},{3,1},{4,6},{5,7},{6,4},{7,5},{8,10},{9,11},{10,... | collective-permute-start | bytes 786440 | tf_op jit(solution)/shard_map/ppermute | solution.py:132
  7.4 10.3 %collective-permute-start.8 = (bf16[32,4096]{1,0:T(8,128)(2,1)}, bf16[32,4096]{1,0:T(8,128)(2,1)S(1)}, u32[]{:S(2)}, u32[]{:S(2)}) collective-permute-start(bf16[32,4096]{1,0:T(8,128)(2,1)} %get-tuple-element.32), channel_id=1, source_target_pairs={{0,4},{1,5},{2,6},{3,7},{4,0},{5,1},{6,2},{7,3},{8,12},{9,13},{10,... | collective-permute-start | bytes 786440 | tf_op jit(solution)/shard_map/ppermute | solution.py:132
  9.7 16.5 %collective-permute-start.9 = (bf16[32,4096]{1,0:T(8,128)(2,1)}, bf16[32,4096]{1,0:T(8,128)(2,1)S(1)}, u32[]{:S(2)}, u32[]{:S(2)}) collective-permute-start(bf16[32,4096]{1,0:T(8,128)(2,1)} %get-tuple-element.33), channel_id=1, source_target_pairs={{0,6},{1,7},{2,4},{3,5},{4,2},{5,3},{6,0},{7,1},{8,14},{9,15},{10,... | collective-permute-start | bytes 786440 | tf_op jit(solution)/shard_map/ppermute | solution.py:132
  11.1 20.5 %collective-permute-start.2 = (bf16[32,4096]{1,0:T(8,128)(2,1)}, bf16[32,4096]{1,0:T(8,128)(2,1)S(1)}, u32[]{:S(2)}, u32[]{:S(2)}) collective-permute-start(bf16[32,4096]{1,0:T(8,128)(2,1)} %get-tuple-element.27), channel_id=1, source_target_pairs={{0,24},{1,25},{2,26},{3,27},{4,28},{5,29},{6,30},{7,31},{8,16},{9,... | collective-permute-start | bytes 786440 | tf_op jit(solution)/shard_map/ppermute | solution.py:132
  27.1 11.6 %collective-permute-start.10 = (bf16[128,2048]{1,0:T(8,128)(2,1)S(1)}, bf16[128,2048]{1,0:T(8,128)(2,1)S(1)}, u32[]{:S(2)}, u32[]{:S(2)}) collective-permute-start(bf16[128,2048]{1,0:T(8,128)(2,1)S(1)} %get-tuple-element.43), channel_id=1, source_target_pairs={{0,1},{1,0},{2,3},{3,2},{4,5},{5,4},{6,7},{7,6},{8,9},{9,8},{10,11... | collective-permute-start | bytes 1572872 | tf_op jit(solution)/shard_map/ppermute | solution.py:132
  31.6 11.0 %collective-permute-start.4 = (bf16[128,4096]{1,0:T(8,128)(2,1)S(1)}, bf16[128,4096]{1,0:T(8,128)(2,1)S(1)}, u32[]{:S(2)}, u32[]{:S(2)}) collective-permute-start(bf16[128,4096]{1,0:T(8,128)(2,1)S(1)} %constant_dynamic-update-slice_fusion.refs_0_), channel_id=1, source_target_pairs={{2,4},{3,5},{4,2},{5,3},{10,12},{11,13},{12,10},{13,11},{18,20},{1... | collective-permute-start | bytes 3145736 | tf_op jit(solution)/shard_map/ppermute | solution.py:132
  32.3 29.8 %collective-permute-start.3 = (bf16[128,4096]{1,0:T(8,128)(2,1)S(1)}, bf16[128,4096]{1,0:T(8,128)(2,1)S(1)}, u32[]{:S(2)}, u32[]{:S(2)}) collective-permute-start(bf16[128,4096]{1,0:T(8,128)(2,1)S(1)} %constant_dynamic-update-slice_fusion.refs_0_), channel_id=1, source_target_pairs={{0,2},{1,3},{2,0},{3,1},{4,6},{5,7},{6,4},{7,5},{8,10},{9,11},{10,... | collective-permute-start | bytes 3145736 | tf_op jit(solution)/shard_map/ppermute | solution.py:132
  38.7 23.4 %copy-start.2 = (bf16[128,2048]{1,0:T(8,128)(2,1)}, bf16[128,2048]{1,0:T(8,128)(2,1)S(1)}, u32[]{:S(2)}) copy-start(bf16[128,2048]{1,0:T(8,128)(2,1)S(1)} %collective-permute-done.10) | copy-start | bytes 1572868
  39.9 27.1 %collective-permute-start.11 = (bf16[256,2048]{1,0:T(8,128)(2,1)}, bf16[256,2048]{1,0:T(8,128)(2,1)}, u32[]{:S(2)}, u32[]{:S(2)}) collective-permute-start(bf16[256,2048]{1,0:T(8,128)(2,1)} %pad_maximum_fusion), channel_id=1, source_target_pairs={{0,8},{1,9},{2,10},{3,11},{4,12},{5,13},{6,14},{7,15},{8,0},{9,1},... | collective-permute-start | bytes 3145736 | tf_op jit(solution)/shard_map/ppermute | solution.py:132
  40.2 32.1 %collective-permute-start.12 = (bf16[256,2048]{1,0:T(8,128)(2,1)}, bf16[256,2048]{1,0:T(8,128)(2,1)}, u32[]{:S(2)}, u32[]{:S(2)}) collective-permute-start(bf16[256,2048]{1,0:T(8,128)(2,1)} %pad_maximum_fusion), channel_id=1, source_target_pairs={{0,16},{1,17},{2,18},{3,19},{4,20},{5,21},{6,22},{7,23},{8,24},{9,... | collective-permute-start | bytes 3145736 | tf_op jit(solution)/shard_map/ppermute | solution.py:132
  40.4 50.4 %collective-permute-start.13 = (bf16[256,2048]{1,0:T(8,128)(2,1)}, bf16[256,2048]{1,0:T(8,128)(2,1)}, u32[]{:S(2)}, u32[]{:S(2)}) collective-permute-start(bf16[256,2048]{1,0:T(8,128)(2,1)} %pad_maximum_fusion), channel_id=1, source_target_pairs={{0,24},{1,25},{2,26},{3,27},{4,28},{5,29},{6,30},{7,31},{8,16},{9,... | collective-permute-start | bytes 3145736 | tf_op jit(solution)/shard_map/ppermute | solution.py:132
  62.2 31.5 %collective-permute-start.5 = (bf16[128,4096]{1,0:T(8,128)(2,1)S(1)}, bf16[128,4096]{1,0:T(8,128)(2,1)}, u32[]{:S(2)}, u32[]{:S(2)}) collective-permute-start(bf16[128,4096]{1,0:T(8,128)(2,1)S(1)} %collective-permute-done.3.refs_1_), channel_id=1, source_target_pairs={{2,4},{3,5},{4,2},{5,3},{10,12},{11,13},{12,10},{13,11},{18,20},{1... | collective-permute-start | bytes 3145736 | tf_op jit(solution)/shard_map/ppermute | solution.py:132
  63.8 37.2 %collective-permute-start.6 = (bf16[128,4096]{1,0:T(8,128)(2,1)S(1)}, bf16[128,4096]{1,0:T(8,128)(2,1)}, u32[]{:S(2)}, u32[]{:S(2)}) collective-permute-start(bf16[128,4096]{1,0:T(8,128)(2,1)S(1)} %collective-permute-done.4.refs_3_), channel_id=1, source_target_pairs={{2,0},{3,1},{4,6},{5,7},{10,8},{11,9},{12,14},{13,15},{18,16},{19,... | collective-permute-start | bytes 3145736 | tf_op jit(solution)/shard_map/ppermute | solution.py:132
  67.0 26.1 %collective-permute-start.14 = (bf16[128,2048]{1,0:T(8,128)(2,1)S(1)}, bf16[128,2048]{1,0:T(8,128)(2,1)S(1)}, u32[]{:S(2)}, u32[]{:S(2)}) collective-permute-start(bf16[128,2048]{1,0:T(8,128)(2,1)S(1)} %slice.8), channel_id=1, source_target_pairs={{0,6},{1,7},{6,0},{7,1},{8,14},{9,15},{14,8},{15,9},{16,22},{17,23... | collective-permute-start | bytes 1572872 | tf_op jit(solution)/shard_map/ppermute | solution.py:132
  72.3 34.7 %copy-start.1 = (f32[16384]{0:T(1024)S(1)}, f32[16384]{0:T(1024)}, u32[]{:S(2)}) copy-start(f32[16384]{0:T(1024)} %param.5) | copy-start | bytes 196612
  72.3 32.8 %collective-permute-start.16 = (bf16[128,4096]{1,0:T(8,128)(2,1)S(1)}, bf16[128,4096]{1,0:T(8,128)(2,1)S(1)}, u32[]{:S(2)}, u32[]{:S(2)}) collective-permute-start(bf16[128,4096]{1,0:T(8,128)(2,1)S(1)} %constant_dynamic-update-slice_fusion.refs_0_), channel_id=1, source_target_pairs={{0,1},{1,0},{2,3},{3,2},{4,5},{5,4},{6,7},{7,6},{8,9},{9,8},{10,11... | collective-permute-start | bytes 3145736 | tf_op jit(solution)/shard_map/ppermute | solution.py:132
  90.8 15.6 %collective-permute-start.17 = (bf16[128,4096]{1,0:T(8,128)(2,1)S(1)}, bf16[128,4096]{1,0:T(8,128)(2,1)S(1)}, u32[]{:S(2)}, u32[]{:S(2)}) collective-permute-start(bf16[128,4096]{1,0:T(8,128)(2,1)S(1)} %collective-permute-done.3.refs_1_), channel_id=1, source_target_pairs={{0,1},{1,0},{2,3},{3,2},{4,5},{5,4},{6,7},{7,6},{8,9},{9,8},{10,11... | collective-permute-start | bytes 3145736 | tf_op jit(solution)/shard_map/ppermute | solution.py:132
  93.1 13.9 %copy-start = (bf16[1024,2048]{1,0:T(8,128)(2,1)S(1)}, bf16[1024,2048]{1,0:T(8,128)(2,1)}, u32[]{:S(2)}) copy-start(bf16[1024,2048]{1,0:T(8,128)(2,1)} %constant_dynamic-update-slice_fusion.8.col) | copy-start | bytes 12582916
  93.1 13.3 %collective-permute-start.19 = (bf16[128,4096]{1,0:T(8,128)(2,1)S(1)}, bf16[128,4096]{1,0:T(8,128)(2,1)S(1)}, u32[]{:S(2)}, u32[]{:S(2)}) collective-permute-start(bf16[128,4096]{1,0:T(8,128)(2,1)S(1)} %collective-permute-done.4.refs_3_), channel_id=1, source_target_pairs={{0,1},{1,0},{2,3},{3,2},{4,5},{5,4},{6,7},{7,6},{8,9},{9,8},{10,11... | collective-permute-start | bytes 3145736 | tf_op jit(solution)/shard_map/ppermute | solution.py:132
  102.3 4.7 %collective-permute-start.18 = (bf16[128,4096]{1,0:T(8,128)(2,1)S(1)}, bf16[128,4096]{1,0:T(8,128)(2,1)S(1)}, u32[]{:S(2)}, u32[]{:S(2)}) collective-permute-start(bf16[128,4096]{1,0:T(8,128)(2,1)S(1)} %broadcast_select_fusion.refs_2_), channel_id=1, source_target_pairs={{0,1},{1,0},{2,3},{3,2},{4,5},{5,4},{6,7},{7,6},{8,9},{9,8},{10,11... | collective-permute-start | bytes 3145736 | tf_op jit(solution)/shard_map/ppermute | solution.py:132
  104.0 3.0 %collective-permute-start.20 = (bf16[128,2048]{1,0:T(8,128)(2,1)S(1)}, bf16[128,2048]{1,0:T(8,128)(2,1)S(1)}, u32[]{:S(2)}, u32[]{:S(2)}) collective-permute-start(bf16[128,2048]{1,0:T(8,128)(2,1)S(1)} %collective-permute-done.14.refs_4_), channel_id=1, source_target_pairs={{0,1},{1,0},{2,3},{3,2},{4,5},{5,4},{6,7},{7,6},{8,9},{9,8},{10,11... | collective-permute-start | bytes 1572872 | tf_op jit(solution)/shard_map/ppermute | solution.py:132
  105.1 15.0 %collective-permute-start.15 = (bf16[128,2048]{1,0:T(8,128)(2,1)S(1)}, bf16[128,2048]{1,0:T(8,128)(2,1)S(1)}, u32[]{:S(2)}, u32[]{:S(2)}) collective-permute-start(bf16[128,2048]{1,0:T(8,128)(2,1)S(1)} %slice.7), channel_id=1, source_target_pairs={{2,0},{3,1},{4,6},{5,7},{10,8},{11,9},{12,14},{13,15},{18,16},{19,... | collective-permute-start | bytes 1572872 | tf_op jit(solution)/shard_map/ppermute | solution.py:132
  120.1 2.8 %collective-permute-start.21 = (bf16[128,2048]{1,0:T(8,128)(2,1)S(1)}, bf16[128,2048]{1,0:T(8,128)(2,1)S(1)}, u32[]{:S(2)}, u32[]{:S(2)}) collective-permute-start(bf16[128,2048]{1,0:T(8,128)(2,1)S(1)} %collective-permute-done.15.refs_4_), channel_id=1, source_target_pairs={{0,1},{1,0},{2,3},{3,2},{4,5},{5,4},{6,7},{7,6},{8,9},{9,8},{10,11... | collective-permute-start | bytes 1572872 | tf_op jit(solution)/shard_map/ppermute | solution.py:132

commit v4 on v3

--- a/solution.py
+++ b/solution.py
@@ -102,7 +102,7 @@
         + ([] if block is None else [pl.BlockSpec(memory_space=pl.ANY)]),
         out_specs=pl.BlockSpec((rows, cols), lambda i: (first // rows + i, 0)),
         input_output_aliases={} if block is None else {2 + count: 0},
-        compiler_params=pltpu.CompilerParams(vmem_limit_bytes=40 << 20),
+        compiler_params=pltpu.CompilerParams(vmem_limit_bytes=28 << 20),
         cost_estimate=pl.CostEstimate(flops=0, bytes_accessed=0, transcendentals=0),
         name="product",
     )(col, damp, *parts, *([] if block is None else [block]))
@@ -168,7 +168,6 @@
         return [value[:, i:j] for i, j in zip(cuts, cuts[1:])]
 
     if planes == 4 and lines == 4:
-        inner = (plane == 1) | (plane == 2)
         near = across_planes(own, 1)
         mid = swap_inner(own)
         col_lines = [mine, across_lines(mine, 1), across_lines(mine, 2)]
@@ -177,16 +176,15 @@
         far_in = swap_inner(near)
         far_out = push_out(mid)
         third = across_lines(mine, 3)
-        first_own = after(cut(own)[0], near, mid)
+        first_own = after(cut(own)[0], near)
         direct = send(first_own, lambda r, q, c: (r, q ^ 3, c) if q in (0, 3) else None)
-        held = jnp.concatenate([mine, one, two], axis=0)
+        held = jnp.concatenate(lax.optimization_barrier((mine, one, two)), axis=0)
         col_panel = jnp.concatenate([held, third], axis=0)
         far_in, far_out, col_panel, direct = lax.optimization_barrier(
             (far_in, far_out, col_panel, direct)
         )
         last = [direct, push_out(cut(far_in)[1])]
-        far = jnp.where(inner, far_in, far_out)
-        slots = [[p] for p in (own, near, far, mid)]
+        slots = [[own], [near], [far_in, far_out], [mid]]
     else:
         col_lines = [mine] + [across_lines(mine, m) for m in range(1, lines)]
         col_panel = jnp.concatenate(col_lines, axis=0)

time: 137 us -> 135 us (0.985)
  waiting for transfers between devices: 43.3 us -> 68.2 us
  starting transfers between devices: 50 us -> 34.9 us
  local copies, waits for them, and re-layouts: 12 us -> 1.37 us
  other arithmetic: 2.52 us -> 0.76 us
    ppermute x22 -> x23, waiting for transfers between devices: 43.3 us -> 68.2 us  [send(): return lax.ppermute(value, AXES, flat)]
    ppermute x22 -> x23, starting transfers between devices: 50 us -> 34.9 us  [send(): return lax.ppermute(value, AXES, flat)]
    unnamed x15 -> x7, local copies, waits for them, and re-layouts: 8.59 us -> 1.14 us
    concatenate x1 -> x0, local copies, waits for them, and re-layouts: 2.3 us -> none  [shards(): col_panel = jnp.concatenate([held, third], axis=0)]
  transfers between devices with their start and end apart: 22 -> 23, of which waited for: 9 -> 10; matrix products, arithmetic and copies ran while one was open for 11% -> 2% of each run, Pallas kernels for 9% -> 9%
where the time goes in v4:
time: 135 us; the launch traced here: 134 us
  waiting for transfers between devices  68.2 us (51%)
  starting transfers between devices  34.9 us (26%)
  Pallas kernels  29.1 us (22%)
  local copies, waits for them, and re-layouts  1.37 us (1%)
    ppermute x23, waiting for transfers between devices, send(): return lax.ppermute(value, AXES, flat)  68.2 us
    ppermute x23, starting transfers between devices, send(): return lax.ppermute(value, AXES, flat)  34.9 us
    pallas_call x2, Pallas kernels, product(): pl.pallas_call(functools.partial(product_kernel, picks, lines, total, fir...  26.3 us
    pallas_call x1, Pallas kernels, pick_panels(): pl.pallas_call(functools.partial(pick_kernel, lines), out_shape=[jax.Shap...  2.78 us
  transfers between devices with their start and end apart: 23, of which 10 were waited for; matrix products, arithmetic and copies ran while one was open for 2% of the time, Pallas kernels for 9%

profile of v4, /device:TPU:1, one launch (start us, length us, event | category | flops | bytes accessed | tf_op | source)
XLA Modules:
  0.0 134.4 jit_solution(1449750205774740848)
XLA Ops:
  0.0 2.8 %pick_panels.1 = (bf16[32,4096]{1,0:T(8,128)(2,1)}, bf16[32,4096]{1,0:T(8,128)(2,1)}, bf16[32,4096]{1,0:T(8,128)(2,1)}, bf16[32,4096]{1,0:T(8,128)(2,1)}, bf16[3...) custom-call(s32[1,16]{1,0:T(1,128)} %mask.1, ...), custom_call_target="tpu_custom_call" | custom-call | tf_op jit(solution)/shard_map/pick_panels/pallas_call | solution.py:38
  2.8 2.0 %collective-permute-start = (bf16[32,4096]{1,0:T(8,128)(2,1)}, bf16[32,4096]{1,0:T(8,128)(2,1)S(1)}, u32[]{:S(2)}, u32[]{:S(2)}) collective-permute-start(bf16[32,4096]{1,0:T(8,128)(2,1)} %get-tuple-element.27), channel_id=1, source_target_pairs={{0,8},{1,9},{2,10},{3,11},{4,12},{5,13},{6,14},{7,15},{8,0},{9,1},... | collective-permute-start | bytes 786440 | tf_op jit(solution)/shard_map/ppermute | solution.py:132
  4.8 1.2 collective-permute-start.1
  6.1 1.3 collective-permute-start.7
  7.4 2.3 %collective-permute-start.8 = (bf16[32,4096]{1,0:T(8,128)(2,1)}, bf16[32,4096]{1,0:T(8,128)(2,1)S(1)}, u32[]{:S(2)}, u32[]{:S(2)}) collective-permute-start(bf16[32,4096]{1,0:T(8,128)(2,1)} %get-tuple-element.35), channel_id=1, source_target_pairs={{0,4},{1,5},{2,6},{3,7},{4,0},{5,1},{6,2},{7,3},{8,12},{9,13},{10,... | collective-permute-start | bytes 786440 | tf_op jit(solution)/shard_map/ppermute | solution.py:132
  9.7 0.0 collective-permute-start.9
  9.7 1.1 constant_dynamic-update-slice_fusion.3
  10.7 0.3 collective-permute-done
  11.1 2.1 %collective-permute-start.2 = (bf16[32,4096]{1,0:T(8,128)(2,1)}, bf16[32,4096]{1,0:T(8,128)(2,1)S(1)}, u32[]{:S(2)}, u32[]{:S(2)}) collective-permute-start(bf16[32,4096]{1,0:T(8,128)(2,1)} %get-tuple-element.30), channel_id=1, source_target_pairs={{0,24},{1,25},{2,26},{3,27},{4,28},{5,29},{6,30},{7,31},{8,16},{9,... | collective-permute-start | bytes 786440 | tf_op jit(solution)/shard_map/ppermute | solution.py:132
  13.2 3.8 %collective-permute-done.7 = bf16[32,4096]{1,0:T(8,128)(2,1)S(1)} collective-permute-done((bf16[32,4096]{1,0:T(8,128)(2,1)}, bf16[32,4096]{1,0:T(8,128)(2,1)S(1)}, u32[]{:S(2)}, u32[]{:S(2)}) %collective-permute-start.7) | collective-permute-done | bytes 262176 | tf_op jit(solution)/shard_map/ppermute | solution.py:132
  17.0 0.7 collective-permute-done.8
  17.7 0.0 copy-start
  17.7 8.4 %collective-permute-done.9 = bf16[32,4096]{1,0:T(8,128)(2,1)S(1)} collective-permute-done((bf16[32,4096]{1,0:T(8,128)(2,1)}, bf16[32,4096]{1,0:T(8,128)(2,1)S(1)}, u32[]{:S(2)}, u32[]{:S(2)}) %collective-permute-start.9) | collective-permute-done | bytes 262176 | tf_op jit(solution)/shard_map/ppermute | solution.py:132
  26.2 0.1 constant_dynamic-slice_fusion.1
  26.3 4.4 %collective-permute-start.10 = (bf16[128,2048]{1,0:T(8,128)(2,1)S(1)}, bf16[128,2048]{1,0:T(8,128)(2,1)S(1)}, u32[]{:S(2)}, u32[]{:S(2)}) collective-permute-start(bf16[128,2048]{1,0:T(8,128)(2,1)S(1)} %get-tuple-element.48), channel_id=1, source_target_pairs={{0,1},{1,0},{2,3},{3,2},{4,5},{5,4},{6,7},{7,6},{8,9},{9,8},{10,11... | collective-permute-start | bytes 1572872 | tf_op jit(solution)/shard_map/ppermute | solution.py:132
  30.7 0.0 collective-permute-done.1
  30.8 0.0 collective-permute-done.2
  30.8 0.7 collective-permute-start.4
  31.6 6.4 %collective-permute-start.3 = (bf16[128,4096]{1,0:T(8,128)(2,1)S(1)}, bf16[128,4096]{1,0:T(8,128)(2,1)S(1)}, u32[]{:S(2)}, u32[]{:S(2)}) collective-permute-start(bf16[128,4096]{1,0:T(8,128)(2,1)S(1)} %constant_dynamic-update-slice_fusion.refs_0_), channel_id=1, source_target_pairs={{0,2},{1,3},{2,0},{3,1},{4,6},{5,7},{6,4},{7,5},{8,10},{9,11},{10,... | collective-permute-start | bytes 3145736 | tf_op jit(solution)/shard_map/ppermute | solution.py:132
  38.0 0.0 collective-permute-done.10
  38.0 0.1 pad_maximum_fusion.1
  38.1 0.3 collective-permute-start.13
  38.3 1.2 collective-permute-start.12
  39.6 1.2 collective-permute-start.11
  40.8 0.0 collective-permute-done.4.refs_4_
  40.8 20.5 %collective-permute-done.3.refs_1_ = bf16[128,4096]{1,0:T(8,128)(2,1)S(1)} collective-permute-done((bf16[128,4096]{1,0:T(8,128)(2,1)S(1)}, bf16[128,4096]{1,0:T(8,128)(2,1)S(1)}, u32[]{:S(2)}, u32[]{:S(2)}) %collective-permute-start.3) | collective-permute-done | bytes 1048608 | tf_op jit(solution)/shard_map/ppermute | solution.py:132
  61.3 1.3 collective-permute-start.6
  62.6 0.7 collective-permute-start.5
  63.3 0.0 collective-permute-done.13
  63.3 3.0 %collective-permute-start.14 = (bf16[128,2048]{1,0:T(8,128)(2,1)S(1)}, bf16[128,2048]{1,0:T(8,128)(2,1)S(1)}, u32[]{:S(2)}, u32[]{:S(2)}) collective-permute-start(bf16[128,2048]{1,0:T(8,128)(2,1)S(1)} %slice.8), channel_id=1, source_target_pairs={{0,6},{1,7},{6,0},{7,1},{8,14},{9,15},{14,8},{15,9},{16,22},{17,23... | collective-permute-start | bytes 1572872 | tf_op jit(solution)/shard_map/ppermute | solution.py:132
  66.3 18.8 %collective-permute-done.12 = bf16[256,2048]{1,0:T(8,128)(2,1)S(1)} collective-permute-done((bf16[256,2048]{1,0:T(8,128)(2,1)S(1)}, bf16[256,2048]{1,0:T(8,128)(2,1)S(1)}, u32[]{:S(2)}, u32[]{:S(2)}) %collective-permute-start.12) | collective-permute-done | bytes 1048608 | tf_op jit(solution)/shard_map/ppermute | solution.py:132
  85.1 1.2 collective-permute-start.16
  86.4 0.0 collective-permute-done.11
  86.4 0.0 collective-permute-start.20
  86.4 0.7 pad_maximum_fusion.col
  87.0 0.0 collective-permute-done.14.refs_5_
  87.1 0.6 collective-permute-start.17
  87.6 10.6 %collective-permute-done.6.refs_3_ = bf16[128,4096]{1,0:T(8,128)(2,1)S(1)} collective-permute-done((bf16[128,4096]{1,0:T(8,128)(2,1)S(1)}, bf16[128,4096]{1,0:T(8,128)(2,1)S(1)}, u32[]{:S(2)}, u32[]{:S(2)}) %collective-permute-start.6) | collective-permute-done | bytes 1048608 | tf_op jit(solution)/shard_map/ppermute | solution.py:132
  98.3 0.0 collective-permute-done.5.refs_2_
  98.3 1.7 %collective-permute-start.19 = (bf16[128,4096]{1,0:T(8,128)(2,1)S(1)}, bf16[128,4096]{1,0:T(8,128)(2,1)S(1)}, u32[]{:S(2)}, u32[]{:S(2)}) collective-permute-start(bf16[128,4096]{1,0:T(8,128)(2,1)S(1)} %collective-permute-done.6.refs_3_), channel_id=1, source_target_pairs={{0,1},{1,0},{2,3},{3,2},{4,5},{5,4},{6,7},{7,6},{8,9},{9,8},{10,11... | collective-permute-start | bytes 3145736 | tf_op jit(solution)/shard_map/ppermute | solution.py:132
  100.0 0.0 collective-permute-start.18
  100.0 0.0 collective-permute-done.16.refs_6_
  100.0 0.5 collective-permute-start.21
  100.5 0.0 collective-permute-done.20.refs_10_
  100.5 1.3 collective-permute-start.15
  101.8 0.0 collective-permute-done.17.refs_7_
  101.8 2.7 %collective-permute-done.21.refs_11_ = bf16[128,2048]{1,0:T(8,128)(2,1)S(1)} collective-permute-done((bf16[128,2048]{1,0:T(8,128)(2,1)S(1)}, bf16[128,2048]{1,0:T(8,128)(2,1)S(1)}, u32[]{:S(2)}, u32[]{:S(2)}) %collective-permute-start.21) | collective-permute-done | bytes 524320 | tf_op jit(solution)/shard_map/ppermute | solution.py:132
  104.5 0.0 collective-permute-done.19.refs_9_
  104.5 0.0 collective-permute-done.18.refs_8_
  104.5 0.0 copy-done
  104.5 12.3 %product.2.refs_12_ = f32[4096,2048]{1,0:T(8,128)} custom-call(bf16[1024,2048]{1,0:T(8,128)(2,1)S(1)} %pad_maximum_fusion.col, f32[1,16384]{1,0:T(1,128)S(1)} %bitcast.1, bf16[128,4096]{1,0:T(8,128)(2,1)S(1)} %constant_dynamic-update-slice_fusion.refs_0_, bf16[128,4096]{1,0:T(8,128)(2,1)S(1)} %collective-permute-done.3.refs_1_, ...), custom_call_target="tpu_custom_call" | custom-call | tf_op jit(solution)/shard_map/product/pallas_call | solution.py:90
  116.8 0.8 collective-permute-done.15.refs_5_
  117.5 1.3 collective-permute-start.22
  118.8 1.5 %collective-permute-done.22.refs_11_ = bf16[128,2048]{1,0:T(8,128)(2,1)S(1)} collective-permute-done((bf16[128,2048]{1,0:T(8,128)(2,1)S(1)}, bf16[128,2048]{1,0:T(8,128)(2,1)S(1)}, u32[]{:S(2)}, u32[]{:S(2)}) %collective-permute-start.22) | collective-permute-done | bytes 524320 | tf_op jit(solution)/shard_map/ppermute | solution.py:132
  120.4 14.0 %product.3 = f32[4096,2048]{1,0:T(8,128)} custom-call(bf16[1024,2048]{1,0:T(8,128)(2,1)S(1)} %pad_maximum_fusion.col, f32[1,16384]{1,0:T(1,128)S(1)} %bitcast.2, bf16[128,4096]{1,0:T(8,128)(2,1)S(1)} %constant_dynamic-update-slice_fusion.refs_0_, bf16[128,4096]{1,0:T(8,128)(2,1)S(1)} %collective-permute-done.3.refs_1_, ...), custom_call_target="tpu_custom_call", output_to_operand_aliasing={{}: (14, {})} | custom-call | tf_op jit(solution)/shard_map/product/pallas_call | solution.py:90
  (8 shorter events, 0.2 us)
Async XLA Ops:
  2.8 8.3 %collective-permute-start = (bf16[32,4096]{1,0:T(8,128)(2,1)}, bf16[32,4096]{1,0:T(8,128)(2,1)S(1)}, u32[]{:S(2)}, u32[]{:S(2)}) collective-permute-start(bf16[32,4096]{1,0:T(8,128)(2,1)} %get-tuple-element.27), channel_id=1, source_target_pairs={{0,8},{1,9},{2,10},{3,11},{4,12},{5,13},{6,14},{7,15},{8,0},{9,1},... | collective-permute-start | bytes 786440 | tf_op jit(solution)/shard_map/ppermute | solution.py:132
  4.8 25.9 %collective-permute-start.1 = (bf16[32,4096]{1,0:T(8,128)(2,1)}, bf16[32,4096]{1,0:T(8,128)(2,1)S(1)}, u32[]{:S(2)}, u32[]{:S(2)}) collective-permute-start(bf16[32,4096]{1,0:T(8,128)(2,1)} %get-tuple-element.28), channel_id=1, source_target_pairs={{0,16},{1,17},{2,18},{3,19},{4,20},{5,21},{6,22},{7,23},{8,24},{9,... | collective-permute-start | bytes 786440 | tf_op jit(solution)/shard_map/ppermute | solution.py:132
  6.1 10.9 %collective-permute-start.7 = (bf16[32,4096]{1,0:T(8,128)(2,1)}, bf16[32,4096]{1,0:T(8,128)(2,1)S(1)}, u32[]{:S(2)}, u32[]{:S(2)}) collective-permute-start(bf16[32,4096]{1,0:T(8,128)(2,1)} %get-tuple-element.34), channel_id=1, source_target_pairs={{0,2},{1,3},{2,0},{3,1},{4,6},{5,7},{6,4},{7,5},{8,10},{9,11},{10,... | collective-permute-start | bytes 786440 | tf_op jit(solution)/shard_map/ppermute | solution.py:132
  7.4 10.3 %collective-permute-start.8 = (bf16[32,4096]{1,0:T(8,128)(2,1)}, bf16[32,4096]{1,0:T(8,128)(2,1)S(1)}, u32[]{:S(2)}, u32[]{:S(2)}) collective-permute-start(bf16[32,4096]{1,0:T(8,128)(2,1)} %get-tuple-element.35), channel_id=1, source_target_pairs={{0,4},{1,5},{2,6},{3,7},{4,0},{5,1},{6,2},{7,3},{8,12},{9,13},{10,... | collective-permute-start | bytes 786440 | tf_op jit(solution)/shard_map/ppermute | solution.py:132
  9.7 16.5 %collective-permute-start.9 = (bf16[32,4096]{1,0:T(8,128)(2,1)}, bf16[32,4096]{1,0:T(8,128)(2,1)S(1)}, u32[]{:S(2)}, u32[]{:S(2)}) collective-permute-start(bf16[32,4096]{1,0:T(8,128)(2,1)} %get-tuple-element.36), channel_id=1, source_target_pairs={{0,6},{1,7},{2,4},{3,5},{4,2},{5,3},{6,0},{7,1},{8,14},{9,15},{10,... | collective-permute-start | bytes 786440 | tf_op jit(solution)/shard_map/ppermute | solution.py:132
  11.1 19.7 %collective-permute-start.2 = (bf16[32,4096]{1,0:T(8,128)(2,1)}, bf16[32,4096]{1,0:T(8,128)(2,1)S(1)}, u32[]{:S(2)}, u32[]{:S(2)}) collective-permute-start(bf16[32,4096]{1,0:T(8,128)(2,1)} %get-tuple-element.30), channel_id=1, source_target_pairs={{0,24},{1,25},{2,26},{3,27},{4,28},{5,29},{6,30},{7,31},{8,16},{9,... | collective-permute-start | bytes 786440 | tf_op jit(solution)/shard_map/ppermute | solution.py:132
  17.7 86.8 %copy-start = (f32[16384]{0:T(1024)S(1)}, f32[16384]{0:T(1024)}, u32[]{:S(2)}) copy-start(f32[16384]{0:T(1024)} %param.5) | copy-start | bytes 196612
  26.3 11.7 %collective-permute-start.10 = (bf16[128,2048]{1,0:T(8,128)(2,1)S(1)}, bf16[128,2048]{1,0:T(8,128)(2,1)S(1)}, u32[]{:S(2)}, u32[]{:S(2)}) collective-permute-start(bf16[128,2048]{1,0:T(8,128)(2,1)S(1)} %get-tuple-element.48), channel_id=1, source_target_pairs={{0,1},{1,0},{2,3},{3,2},{4,5},{5,4},{6,7},{7,6},{8,9},{9,8},{10,11... | collective-permute-start | bytes 1572872 | tf_op jit(solution)/shard_map/ppermute | solution.py:132
  30.8 10.0 %collective-permute-start.4 = (bf16[128,4096]{1,0:T(8,128)(2,1)S(1)}, bf16[128,4096]{1,0:T(8,128)(2,1)S(1)}, u32[]{:S(2)}, u32[]{:S(2)}) collective-permute-start(bf16[128,4096]{1,0:T(8,128)(2,1)S(1)} %constant_dynamic-update-slice_fusion.refs_0_), channel_id=1, source_target_pairs={{2,4},{3,5},{4,2},{5,3},{10,12},{11,13},{12,10},{13,11},{18,20},{1... | collective-permute-start | bytes 3145736 | tf_op jit(solution)/shard_map/ppermute | solution.py:132
  31.6 29.7 %collective-permute-start.3 = (bf16[128,4096]{1,0:T(8,128)(2,1)S(1)}, bf16[128,4096]{1,0:T(8,128)(2,1)S(1)}, u32[]{:S(2)}, u32[]{:S(2)}) collective-permute-start(bf16[128,4096]{1,0:T(8,128)(2,1)S(1)} %constant_dynamic-update-slice_fusion.refs_0_), channel_id=1, source_target_pairs={{0,2},{1,3},{2,0},{3,1},{4,6},{5,7},{6,4},{7,5},{8,10},{9,11},{10,... | collective-permute-start | bytes 3145736 | tf_op jit(solution)/shard_map/ppermute | solution.py:132
  38.1 25.3 %collective-permute-start.13 = (bf16[256,2048]{1,0:T(8,128)(2,1)S(1)}, bf16[256,2048]{1,0:T(8,128)(2,1)S(1)}, u32[]{:S(2)}, u32[]{:S(2)}) collective-permute-start(bf16[256,2048]{1,0:T(8,128)(2,1)S(1)} %pad_maximum_fusion.1), channel_id=1, source_target_pairs={{0,24},{1,25},{2,26},{3,27},{4,28},{5,29},{6,30},{7,31},{8,16},{9,... | collective-permute-start | bytes 3145736 | tf_op jit(solution)/shard_map/ppermute | solution.py:132
  38.3 46.8 %collective-permute-start.12 = (bf16[256,2048]{1,0:T(8,128)(2,1)S(1)}, bf16[256,2048]{1,0:T(8,128)(2,1)S(1)}, u32[]{:S(2)}, u32[]{:S(2)}) collective-permute-start(bf16[256,2048]{1,0:T(8,128)(2,1)S(1)} %pad_maximum_fusion.1), channel_id=1, source_target_pairs={{0,16},{1,17},{2,18},{3,19},{4,20},{5,21},{6,22},{7,23},{8,24},{9,... | collective-permute-start | bytes 3145736 | tf_op jit(solution)/shard_map/ppermute | solution.py:132
  39.6 46.8 %collective-permute-start.11 = (bf16[256,2048]{1,0:T(8,128)(2,1)S(1)}, bf16[256,2048]{1,0:T(8,128)(2,1)S(1)}, u32[]{:S(2)}, u32[]{:S(2)}) collective-permute-start(bf16[256,2048]{1,0:T(8,128)(2,1)S(1)} %pad_maximum_fusion.1), channel_id=1, source_target_pairs={{0,8},{1,9},{2,10},{3,11},{4,12},{5,13},{6,14},{7,15},{8,0},{9,1},... | collective-permute-start | bytes 3145736 | tf_op jit(solution)/shard_map/ppermute | solution.py:132
  61.3 37.0 %collective-permute-start.6 = (bf16[128,4096]{1,0:T(8,128)(2,1)S(1)}, bf16[128,4096]{1,0:T(8,128)(2,1)S(1)}, u32[]{:S(2)}, u32[]{:S(2)}) collective-permute-start(bf16[128,4096]{1,0:T(8,128)(2,1)S(1)} %collective-permute-done.4.refs_4_), channel_id=1, source_target_pairs={{2,0},{3,1},{4,6},{5,7},{10,8},{11,9},{12,14},{13,15},{18,16},{19,... | collective-permute-start | bytes 3145736 | tf_op jit(solution)/shard_map/ppermute | solution.py:132
  62.6 35.7 %collective-permute-start.5 = (bf16[128,4096]{1,0:T(8,128)(2,1)S(1)}, bf16[128,4096]{1,0:T(8,128)(2,1)S(1)}, u32[]{:S(2)}, u32[]{:S(2)}) collective-permute-start(bf16[128,4096]{1,0:T(8,128)(2,1)S(1)} %collective-permute-done.3.refs_1_), channel_id=1, source_target_pairs={{2,4},{3,5},{4,2},{5,3},{10,12},{11,13},{12,10},{13,11},{18,20},{1... | collective-permute-start | bytes 3145736 | tf_op jit(solution)/shard_map/ppermute | solution.py:132
  63.3 23.7 %collective-permute-start.14 = (bf16[128,2048]{1,0:T(8,128)(2,1)S(1)}, bf16[128,2048]{1,0:T(8,128)(2,1)S(1)}, u32[]{:S(2)}, u32[]{:S(2)}) collective-permute-start(bf16[128,2048]{1,0:T(8,128)(2,1)S(1)} %slice.8), channel_id=1, source_target_pairs={{0,6},{1,7},{6,0},{7,1},{8,14},{9,15},{14,8},{15,9},{16,22},{17,23... | collective-permute-start | bytes 1572872 | tf_op jit(solution)/shard_map/ppermute | solution.py:132
  85.1 14.8 %collective-permute-start.16 = (bf16[128,4096]{1,0:T(8,128)(2,1)S(1)}, bf16[128,4096]{1,0:T(8,128)(2,1)S(1)}, u32[]{:S(2)}, u32[]{:S(2)}) collective-permute-start(bf16[128,4096]{1,0:T(8,128)(2,1)S(1)} %constant_dynamic-update-slice_fusion.refs_0_), channel_id=1, source_target_pairs={{0,1},{1,0},{2,3},{3,2},{4,5},{5,4},{6,7},{7,6},{8,9},{9,8},{10,11... | collective-permute-start | bytes 3145736 | tf_op jit(solution)/shard_map/ppermute | solution.py:132
  86.4 14.2 %collective-permute-start.20 = (bf16[128,4096]{1,0:T(8,128)(2,1)S(1)}, bf16[128,4096]{1,0:T(8,128)(2,1)S(1)}, u32[]{:S(2)}, u32[]{:S(2)}) collective-permute-start(bf16[128,4096]{1,0:T(8,128)(2,1)S(1)} %collective-permute-done.4.refs_4_), channel_id=1, source_target_pairs={{0,1},{1,0},{2,3},{3,2},{4,5},{5,4},{6,7},{7,6},{8,9},{9,8},{10,11... | collective-permute-start | bytes 3145736 | tf_op jit(solution)/shard_map/ppermute | solution.py:132
  87.1 14.8 %collective-permute-start.17 = (bf16[128,4096]{1,0:T(8,128)(2,1)S(1)}, bf16[128,4096]{1,0:T(8,128)(2,1)S(1)}, u32[]{:S(2)}, u32[]{:S(2)}) collective-permute-start(bf16[128,4096]{1,0:T(8,128)(2,1)S(1)} %collective-permute-done.3.refs_1_), channel_id=1, source_target_pairs={{0,1},{1,0},{2,3},{3,2},{4,5},{5,4},{6,7},{7,6},{8,9},{9,8},{10,11... | collective-permute-start | bytes 3145736 | tf_op jit(solution)/shard_map/ppermute | solution.py:132
  98.3 6.2 %collective-permute-start.19 = (bf16[128,4096]{1,0:T(8,128)(2,1)S(1)}, bf16[128,4096]{1,0:T(8,128)(2,1)S(1)}, u32[]{:S(2)}, u32[]{:S(2)}) collective-permute-start(bf16[128,4096]{1,0:T(8,128)(2,1)S(1)} %collective-permute-done.6.refs_3_), channel_id=1, source_target_pairs={{0,1},{1,0},{2,3},{3,2},{4,5},{5,4},{6,7},{7,6},{8,9},{9,8},{10,11... | collective-permute-start | bytes 3145736 | tf_op jit(solution)/shard_map/ppermute | solution.py:132
  100.0 4.5 %collective-permute-start.18 = (bf16[128,4096]{1,0:T(8,128)(2,1)S(1)}, bf16[128,4096]{1,0:T(8,128)(2,1)S(1)}, u32[]{:S(2)}, u32[]{:S(2)}) collective-permute-start(bf16[128,4096]{1,0:T(8,128)(2,1)S(1)} %collective-permute-done.5.refs_2_), channel_id=1, source_target_pairs={{0,1},{1,0},{2,3},{3,2},{4,5},{5,4},{6,7},{7,6},{8,9},{9,8},{10,11... | collective-permute-start | bytes 3145736 | tf_op jit(solution)/shard_map/ppermute | solution.py:132
  100.0 4.5 %collective-permute-start.21 = (bf16[128,2048]{1,0:T(8,128)(2,1)S(1)}, bf16[128,2048]{1,0:T(8,128)(2,1)S(1)}, u32[]{:S(2)}, u32[]{:S(2)}) collective-permute-start(bf16[128,2048]{1,0:T(8,128)(2,1)S(1)} %collective-permute-done.14.refs_5_), channel_id=1, source_target_pairs={{0,1},{1,0},{2,3},{3,2},{4,5},{5,4},{6,7},{7,6},{8,9},{9,8},{10,11... | collective-permute-start | bytes 1572872 | tf_op jit(solution)/shard_map/ppermute | solution.py:132
  100.5 17.0 %collective-permute-start.15 = (bf16[128,2048]{1,0:T(8,128)(2,1)S(1)}, bf16[128,2048]{1,0:T(8,128)(2,1)S(1)}, u32[]{:S(2)}, u32[]{:S(2)}) collective-permute-start(bf16[128,2048]{1,0:T(8,128)(2,1)S(1)} %slice.7), channel_id=1, source_target_pairs={{2,0},{3,1},{4,6},{5,7},{10,8},{11,9},{12,14},{13,15},{18,16},{19,... | collective-permute-start | bytes 1572872 | tf_op jit(solution)/shard_map/ppermute | solution.py:132
  117.5 2.8 %collective-permute-start.22 = (bf16[128,2048]{1,0:T(8,128)(2,1)S(1)}, bf16[128,2048]{1,0:T(8,128)(2,1)S(1)}, u32[]{:S(2)}, u32[]{:S(2)}) collective-permute-start(bf16[128,2048]{1,0:T(8,128)(2,1)S(1)} %collective-permute-done.15.refs_5_), channel_id=1, source_target_pairs={{0,1},{1,0},{2,3},{3,2},{4,5},{5,4},{6,7},{7,6},{8,9},{9,8},{10,11... | collective-permute-start | bytes 1572872 | tf_op jit(solution)/shard_map/ppermute | solution.py:132

commit v5 on v4

--- a/solution.py
+++ b/solution.py
@@ -18,14 +18,13 @@
     return lax.optimization_barrier((value,) + others)[0]
 
 
-def pick_kernel(lines, mask, slab, *outs):
-    line = lax.axis_index("row")
-    plane = lax.axis_index("col") // CORES
+def pick_kernel(axis, mask, slab, *outs):
+    place = lax.axis_index("row") if axis == "row" else lax.axis_index("col") // CORES
     span = slab.shape[1] // mask.shape[1]
     for slot, out in enumerate(outs):
         width = out.shape[1]
         step = min(width, span)
-        panel = line ^ slot if slot < lines else plane ^ (slot - lines)
+        panel = place ^ slot
         for part in range(width // step):
             start = pl.multiple_of(panel * width + part * step, step)
             keep = mask[0, start // span]
@@ -33,16 +32,16 @@
             out[:, part * step : (part + 1) * step] = jnp.where(keep != 0, piece, jnp.zeros_like(piece))
 
 
-def pick_panels(slab, mask, lines, planes):
+def pick_panels(slab, mask, axis, count):
     rows, width = slab.shape
     return pl.pallas_call(
-        functools.partial(pick_kernel, lines),
-        out_shape=[jax.ShapeDtypeStruct((rows, width // lines), slab.dtype)] * (lines + planes),
+        functools.partial(pick_kernel, axis),
+        out_shape=[jax.ShapeDtypeStruct((rows, width // count), slab.dtype)] * count,
         in_specs=[
             pl.BlockSpec(memory_space=pltpu.SMEM),
             pl.BlockSpec(memory_space=pltpu.VMEM),
         ],
-        out_specs=[pl.BlockSpec(memory_space=pltpu.VMEM)] * (lines + planes),
+        out_specs=[pl.BlockSpec(memory_space=pltpu.VMEM)] * count,
         name="pick_panels",
     )(mask, slab)
 
@@ -146,13 +145,13 @@
     def push_out(value):
         return send(value, lambda r, q, c: (r, q ^ 1, c) if q in (1, 2) else None)
 
-    picked = pick_panels(slab, block_mask, lines, planes)
-    by_line, by_plane = picked[:lines], picked[lines:]
+    by_plane = pick_panels(slab, block_mask, "col", planes)
+    by_line = pick_panels(after(slab, by_plane[0]), block_mask, "row", lines)
 
     col_parts = [by_plane[0]] + [across_planes(by_plane[k], k) for k in range(planes - 1, 0, -1)][::-1]
     row_parts = [by_line[0]]
     for m in range(1, lines):
-        row_parts.append(across_lines(after(by_line[m], *row_parts[1:2]) if m == 3 else by_line[m], m))
+        row_parts.append(across_lines(by_line[m], m))
     mine = jnp.concatenate(col_parts, axis=0)
     keep = lax.dynamic_slice_in_dim(mine, core * half, half, 1)
     give = lax.dynamic_slice_in_dim(mine, (1 - core) * half, half, 1)

time: 135 us -> 133 us (0.985)
  waiting for transfers between devices: 68.2 us -> 63.9 us
  Pallas kernels: 29.1 us -> 31 us
  starting transfers between devices: 34.9 us -> 33.4 us
    ppermute x23, waiting for transfers between devices: 68.2 us -> 63.9 us  [send(): return lax.ppermute(value, AXES, flat)]
    pallas_call x1 -> x2, Pallas kernels: 2.78 us -> 4.67 us  [pick_panels(): pl.pallas_call(functools.partial(pick_kernel, axis), out_shape=[jax.Shape...]
    ppermute x23, starting transfers between devices: 34.9 us -> 33.4 us  [send(): return lax.ppermute(value, AXES, flat)]
  transfers between devices with their start and end apart: 23 -> 23, of which waited for: 10 -> 8; matrix products, arithmetic and copies ran while one was open for 2% -> 2% of each run, Pallas kernels for 9% -> 11%
where the time goes in v5:
time: 133 us; the launch traced here: 131 us
  waiting for transfers between devices  63.9 us (48%)
  starting transfers between devices  33.4 us (25%)
  Pallas kernels  31 us (23%)
  local copies, waits for them, and re-layouts  2.21 us (2%)
    ppermute x23, waiting for transfers between devices, send(): return lax.ppermute(value, AXES, flat)  63.9 us
    ppermute x23, starting transfers between devices, send(): return lax.ppermute(value, AXES, flat)  33.4 us
    pallas_call x2, Pallas kernels, product(): pl.pallas_call(functools.partial(product_kernel, picks, lines, total, fir...  26.3 us
    pallas_call x2, Pallas kernels, pick_panels(): pl.pallas_call(functools.partial(pick_kernel, axis), out_shape=[jax.Shape...  4.67 us
  transfers between devices with their start and end apart: 23, of which 8 were waited for; matrix products, arithmetic and copies ran while one was open for 2% of the time, Pallas kernels for 11%

profile of v5, /device:TPU:1, one launch (start us, length us, event | category | flops | bytes accessed | tf_op | source)
XLA Modules:
  0.0 131.4 jit_solution(13421727581887236153)
XLA Ops:
  0.0 2.3 %pick_panels.2 = (bf16[32,4096]{1,0:T(8,128)(2,1)}, bf16[32,4096]{1,0:T(8,128)(2,1)}, bf16[32,4096]{1,0:T(8,128)(2,1)}, bf16[32,4096]{1,0:T(8,128)(2,1)}) custom-call(s32[1,16]{1,0:T(1,128)} %mask.3, bf16[32,16384]{1,0:T(8,128)(2,1)} %slab.2), custom_call_target="tpu_custom_call" | custom-call | tf_op jit(solution)/shard_map/pick_panels/pallas_call | solution.py:37
  2.3 2.1 %collective-permute-start.7 = (bf16[32,4096]{1,0:T(8,128)(2,1)}, bf16[32,4096]{1,0:T(8,128)(2,1)S(1)}, u32[]{:S(2)}, u32[]{:S(2)}) collective-permute-start(bf16[32,4096]{1,0:T(8,128)(2,1)} %get-tuple-element.34), channel_id=1, source_target_pairs={{0,2},{1,3},{2,0},{3,1},{4,6},{5,7},{6,4},{7,5},{8,10},{9,11},{10,... | collective-permute-start | bytes 786440 | tf_op jit(solution)/shard_map/ppermute | solution.py:131
  4.4 2.3 %collective-permute-start.8 = (bf16[32,4096]{1,0:T(8,128)(2,1)}, bf16[32,4096]{1,0:T(8,128)(2,1)S(1)}, u32[]{:S(2)}, u32[]{:S(2)}) collective-permute-start(bf16[32,4096]{1,0:T(8,128)(2,1)} %get-tuple-element.35), channel_id=1, source_target_pairs={{0,4},{1,5},{2,6},{3,7},{4,0},{5,1},{6,2},{7,3},{8,12},{9,13},{10,... | collective-permute-start | bytes 786440 | tf_op jit(solution)/shard_map/ppermute | solution.py:131
  6.7 0.0 collective-permute-start.9
  6.7 2.4 %pick_panels.3 = (bf16[32,4096]{1,0:T(8,128)(2,1)}, bf16[32,4096]{1,0:T(8,128)(2,1)}, bf16[32,4096]{1,0:T(8,128)(2,1)}, bf16[32,4096]{1,0:T(8,128)(2,1)}) custom-call(s32[1,16]{1,0:T(1,128)} %mask.3, bf16[32,16384]{1,0:T(8,128)(2,1)} %slab.2), custom_call_target="tpu_custom_call" | custom-call | tf_op jit(solution)/shard_map/pick_panels/pallas_call | solution.py:37
  9.1 1.2 collective-permute-start
  10.3 1.2 collective-permute-start.1
  11.6 1.0 constant_dynamic-update-slice_fusion.7
  12.5 1.0 constant_dynamic-update-slice_fusion.3
  13.5 2.0 %collective-permute-done.7 = bf16[32,4096]{1,0:T(8,128)(2,1)S(1)} collective-permute-done((bf16[32,4096]{1,0:T(8,128)(2,1)}, bf16[32,4096]{1,0:T(8,128)(2,1)S(1)}, u32[]{:S(2)}, u32[]{:S(2)}) %collective-permute-start.7) | collective-permute-done | bytes 262176 | tf_op jit(solution)/shard_map/ppermute | solution.py:131
  15.5 2.0 %collective-permute-start.2 = (bf16[32,4096]{1,0:T(8,128)(2,1)}, bf16[32,4096]{1,0:T(8,128)(2,1)S(1)}, u32[]{:S(2)}, u32[]{:S(2)}) collective-permute-start(bf16[32,4096]{1,0:T(8,128)(2,1)} %get-tuple-element.31), channel_id=1, source_target_pairs={{0,24},{1,25},{2,26},{3,27},{4,28},{5,29},{6,30},{7,31},{8,16},{9,... | collective-permute-start | bytes 786440 | tf_op jit(solution)/shard_map/ppermute | solution.py:131
  17.6 0.0 collective-permute-done.8
  17.6 0.0 copy-start
  17.6 6.2 %collective-permute-done.9 = bf16[32,4096]{1,0:T(8,128)(2,1)S(1)} collective-permute-done((bf16[32,4096]{1,0:T(8,128)(2,1)}, bf16[32,4096]{1,0:T(8,128)(2,1)S(1)}, u32[]{:S(2)}, u32[]{:S(2)}) %collective-permute-start.9) | collective-permute-done | bytes 262176 | tf_op jit(solution)/shard_map/ppermute | solution.py:131
  23.8 0.1 constant_dynamic-slice_fusion.1
  23.9 3.3 %collective-permute-start.10 = (bf16[128,2048]{1,0:T(8,128)(2,1)S(1)}, bf16[128,2048]{1,0:T(8,128)(2,1)S(1)}, u32[]{:S(2)}, u32[]{:S(2)}) collective-permute-start(bf16[128,2048]{1,0:T(8,128)(2,1)S(1)} %get-tuple-element.48), channel_id=1, source_target_pairs={{0,1},{1,0},{2,3},{3,2},{4,5},{5,4},{6,7},{7,6},{8,9},{9,8},{10,11... | collective-permute-start | bytes 1572872 | tf_op jit(solution)/shard_map/ppermute | solution.py:131
  27.2 0.0 collective-permute-done
  27.2 0.0 collective-permute-done.1
  27.3 0.0 collective-permute-done.2
  27.3 0.7 collective-permute-start.4
  28.0 7.0 %collective-permute-start.3 = (bf16[128,4096]{1,0:T(8,128)(2,1)S(1)}, bf16[128,4096]{1,0:T(8,128)(2,1)S(1)}, u32[]{:S(2)}, u32[]{:S(2)}) collective-permute-start(bf16[128,4096]{1,0:T(8,128)(2,1)S(1)} %constant_dynamic-update-slice_fusion.refs_0_), channel_id=1, source_target_pairs={{0,2},{1,3},{2,0},{3,1},{4,6},{5,7},{6,4},{7,5},{8,10},{9,11},{10,... | collective-permute-start | bytes 3145736 | tf_op jit(solution)/shard_map/ppermute | solution.py:131
  35.0 0.0 collective-permute-done.10
  35.0 0.1 pad_maximum_fusion.1
  35.1 2.2 %collective-permute-start.13 = (bf16[256,2048]{1,0:T(8,128)(2,1)S(1)}, bf16[256,2048]{1,0:T(8,128)(2,1)S(1)}, u32[]{:S(2)}, u32[]{:S(2)}) collective-permute-start(bf16[256,2048]{1,0:T(8,128)(2,1)S(1)} %pad_maximum_fusion.1), channel_id=1, source_target_pairs={{0,24},{1,25},{2,26},{3,27},{4,28},{5,29},{6,30},{7,31},{8,16},{9,... | collective-permute-start | bytes 3145736 | tf_op jit(solution)/shard_map/ppermute | solution.py:131
  37.3 0.2 collective-permute-start.12
  37.6 0.3 collective-permute-start.11
  37.8 0.0 collective-permute-done.4.refs_4_
  37.8 20.5 %collective-permute-done.3.refs_1_ = bf16[128,4096]{1,0:T(8,128)(2,1)S(1)} collective-permute-done((bf16[128,4096]{1,0:T(8,128)(2,1)S(1)}, bf16[128,4096]{1,0:T(8,128)(2,1)S(1)}, u32[]{:S(2)}, u32[]{:S(2)}) %collective-permute-start.3) | collective-permute-done | bytes 1048608 | tf_op jit(solution)/shard_map/ppermute | solution.py:131
  58.3 1.3 collective-permute-start.6
  59.6 0.7 collective-permute-start.5
  60.4 0.0 collective-permute-done.13
  60.4 3.0 %collective-permute-start.14 = (bf16[128,2048]{1,0:T(8,128)(2,1)S(1)}, bf16[128,2048]{1,0:T(8,128)(2,1)S(1)}, u32[]{:S(2)}, u32[]{:S(2)}) collective-permute-start(bf16[128,2048]{1,0:T(8,128)(2,1)S(1)} %slice.8), channel_id=1, source_target_pairs={{0,6},{1,7},{6,0},{7,1},{8,14},{9,15},{14,8},{15,9},{16,22},{17,23... | collective-permute-start | bytes 1572872 | tf_op jit(solution)/shard_map/ppermute | solution.py:131
  63.4 20.2 %collective-permute-done.12 = bf16[256,2048]{1,0:T(8,128)(2,1)S(1)} collective-permute-done((bf16[256,2048]{1,0:T(8,128)(2,1)S(1)}, bf16[256,2048]{1,0:T(8,128)(2,1)S(1)}, u32[]{:S(2)}, u32[]{:S(2)}) %collective-permute-start.12) | collective-permute-done | bytes 1048608 | tf_op jit(solution)/shard_map/ppermute | solution.py:131
  83.6 0.5 collective-permute-start.16
  84.1 0.0 collective-permute-done.11
  84.1 0.1 collective-permute-start.20
  84.2 0.7 pad_maximum_fusion.col
  84.9 0.0 collective-permute-done.14.refs_5_
  84.9 0.5 collective-permute-start.17
  85.4 9.9 %collective-permute-done.6.refs_3_ = bf16[128,4096]{1,0:T(8,128)(2,1)S(1)} collective-permute-done((bf16[128,4096]{1,0:T(8,128)(2,1)S(1)}, bf16[128,4096]{1,0:T(8,128)(2,1)S(1)}, u32[]{:S(2)}, u32[]{:S(2)}) %collective-permute-start.6) | collective-permute-done | bytes 1048608 | tf_op jit(solution)/shard_map/ppermute | solution.py:131
  95.3 0.0 collective-permute-done.5.refs_2_
  95.3 1.7 %collective-permute-start.19 = (bf16[128,4096]{1,0:T(8,128)(2,1)S(1)}, bf16[128,4096]{1,0:T(8,128)(2,1)S(1)}, u32[]{:S(2)}, u32[]{:S(2)}) collective-permute-start(bf16[128,4096]{1,0:T(8,128)(2,1)S(1)} %collective-permute-done.6.refs_3_), channel_id=1, source_target_pairs={{0,1},{1,0},{2,3},{3,2},{4,5},{5,4},{6,7},{7,6},{8,9},{9,8},{10,11... | collective-permute-start | bytes 3145736 | tf_op jit(solution)/shard_map/ppermute | solution.py:131
  97.0 0.0 collective-permute-start.18
  97.0 0.0 collective-permute-done.16.refs_6_
  97.0 0.5 collective-permute-start.21
  97.6 0.0 collective-permute-done.20.refs_10_
  97.6 1.3 collective-permute-start.15
  98.9 0.0 collective-permute-done.17.refs_7_
  98.9 2.7 %collective-permute-done.21.refs_11_ = bf16[128,2048]{1,0:T(8,128)(2,1)S(1)} collective-permute-done((bf16[128,2048]{1,0:T(8,128)(2,1)S(1)}, bf16[128,2048]{1,0:T(8,128)(2,1)S(1)}, u32[]{:S(2)}, u32[]{:S(2)}) %collective-permute-start.21) | collective-permute-done | bytes 524320 | tf_op jit(solution)/shard_map/ppermute | solution.py:131
  101.5 0.0 collective-permute-done.19.refs_9_
  101.5 0.0 collective-permute-done.18.refs_8_
  101.5 0.0 copy-done
  101.5 12.3 %product.2.refs_12_ = f32[4096,2048]{1,0:T(8,128)} custom-call(bf16[1024,2048]{1,0:T(8,128)(2,1)S(1)} %pad_maximum_fusion.col, f32[1,16384]{1,0:T(1,128)S(1)} %bitcast.1, bf16[128,4096]{1,0:T(8,128)(2,1)S(1)} %constant_dynamic-update-slice_fusion.refs_0_, bf16[128,4096]{1,0:T(8,128)(2,1)S(1)} %collective-permute-done.3.refs_1_, ...), custom_call_target="tpu_custom_call" | custom-call | tf_op jit(solution)/shard_map/product/pallas_call | solution.py:89
  113.8 0.8 collective-permute-done.15.refs_5_
  114.6 1.3 collective-permute-start.22
  115.9 1.5 %collective-permute-done.22.refs_11_ = bf16[128,2048]{1,0:T(8,128)(2,1)S(1)} collective-permute-done((bf16[128,2048]{1,0:T(8,128)(2,1)S(1)}, bf16[128,2048]{1,0:T(8,128)(2,1)S(1)}, u32[]{:S(2)}, u32[]{:S(2)}) %collective-permute-start.22) | collective-permute-done | bytes 524320 | tf_op jit(solution)/shard_map/ppermute | solution.py:131
  117.4 14.0 %product.3 = f32[4096,2048]{1,0:T(8,128)} custom-call(bf16[1024,2048]{1,0:T(8,128)(2,1)S(1)} %pad_maximum_fusion.col, f32[1,16384]{1,0:T(1,128)S(1)} %bitcast.2, bf16[128,4096]{1,0:T(8,128)(2,1)S(1)} %constant_dynamic-update-slice_fusion.refs_0_, bf16[128,4096]{1,0:T(8,128)(2,1)S(1)} %collective-permute-done.3.refs_1_, ...), custom_call_target="tpu_custom_call", output_to_operand_aliasing={{}: (14, {})} | custom-call | tf_op jit(solution)/shard_map/product/pallas_call | solution.py:89
  (8 shorter events, 0.2 us)
Async XLA Ops:
  2.3 13.2 %collective-permute-start.7 = (bf16[32,4096]{1,0:T(8,128)(2,1)}, bf16[32,4096]{1,0:T(8,128)(2,1)S(1)}, u32[]{:S(2)}, u32[]{:S(2)}) collective-permute-start(bf16[32,4096]{1,0:T(8,128)(2,1)} %get-tuple-element.34), channel_id=1, source_target_pairs={{0,2},{1,3},{2,0},{3,1},{4,6},{5,7},{6,4},{7,5},{8,10},{9,11},{10,... | collective-permute-start | bytes 786440 | tf_op jit(solution)/shard_map/ppermute | solution.py:131
  4.4 13.1 %collective-permute-start.8 = (bf16[32,4096]{1,0:T(8,128)(2,1)}, bf16[32,4096]{1,0:T(8,128)(2,1)S(1)}, u32[]{:S(2)}, u32[]{:S(2)}) collective-permute-start(bf16[32,4096]{1,0:T(8,128)(2,1)} %get-tuple-element.35), channel_id=1, source_target_pairs={{0,4},{1,5},{2,6},{3,7},{4,0},{5,1},{6,2},{7,3},{8,12},{9,13},{10,... | collective-permute-start | bytes 786440 | tf_op jit(solution)/shard_map/ppermute | solution.py:131
  6.7 17.1 %collective-permute-start.9 = (bf16[32,4096]{1,0:T(8,128)(2,1)}, bf16[32,4096]{1,0:T(8,128)(2,1)S(1)}, u32[]{:S(2)}, u32[]{:S(2)}) collective-permute-start(bf16[32,4096]{1,0:T(8,128)(2,1)} %get-tuple-element.36), channel_id=1, source_target_pairs={{0,6},{1,7},{2,4},{3,5},{4,2},{5,3},{6,0},{7,1},{8,14},{9,15},{10,... | collective-permute-start | bytes 786440 | tf_op jit(solution)/shard_map/ppermute | solution.py:131
  9.1 18.1 %collective-permute-start = (bf16[32,4096]{1,0:T(8,128)(2,1)}, bf16[32,4096]{1,0:T(8,128)(2,1)S(1)}, u32[]{:S(2)}, u32[]{:S(2)}) collective-permute-start(bf16[32,4096]{1,0:T(8,128)(2,1)} %get-tuple-element.29), channel_id=1, source_target_pairs={{0,8},{1,9},{2,10},{3,11},{4,12},{5,13},{6,14},{7,15},{8,0},{9,1},... | collective-permute-start | bytes 786440 | tf_op jit(solution)/shard_map/ppermute | solution.py:131
  10.3 16.9 %collective-permute-start.1 = (bf16[32,4096]{1,0:T(8,128)(2,1)}, bf16[32,4096]{1,0:T(8,128)(2,1)S(1)}, u32[]{:S(2)}, u32[]{:S(2)}) collective-permute-start(bf16[32,4096]{1,0:T(8,128)(2,1)} %get-tuple-element.30), channel_id=1, source_target_pairs={{0,16},{1,17},{2,18},{3,19},{4,20},{5,21},{6,22},{7,23},{8,24},{9,... | collective-permute-start | bytes 786440 | tf_op jit(solution)/shard_map/ppermute | solution.py:131
  15.5 11.7 %collective-permute-start.2 = (bf16[32,4096]{1,0:T(8,128)(2,1)}, bf16[32,4096]{1,0:T(8,128)(2,1)S(1)}, u32[]{:S(2)}, u32[]{:S(2)}) collective-permute-start(bf16[32,4096]{1,0:T(8,128)(2,1)} %get-tuple-element.31), channel_id=1, source_target_pairs={{0,24},{1,25},{2,26},{3,27},{4,28},{5,29},{6,30},{7,31},{8,16},{9,... | collective-permute-start | bytes 786440 | tf_op jit(solution)/shard_map/ppermute | solution.py:131
  17.6 83.9 %copy-start = (f32[16384]{0:T(1024)S(1)}, f32[16384]{0:T(1024)}, u32[]{:S(2)}) copy-start(f32[16384]{0:T(1024)} %param.5) | copy-start | bytes 196612
  23.9 11.1 %collective-permute-start.10 = (bf16[128,2048]{1,0:T(8,128)(2,1)S(1)}, bf16[128,2048]{1,0:T(8,128)(2,1)S(1)}, u32[]{:S(2)}, u32[]{:S(2)}) collective-permute-start(bf16[128,2048]{1,0:T(8,128)(2,1)S(1)} %get-tuple-element.48), channel_id=1, source_target_pairs={{0,1},{1,0},{2,3},{3,2},{4,5},{5,4},{6,7},{7,6},{8,9},{9,8},{10,11... | collective-permute-start | bytes 1572872 | tf_op jit(solution)/shard_map/ppermute | solution.py:131
  27.3 10.5 %collective-permute-start.4 = (bf16[128,4096]{1,0:T(8,128)(2,1)S(1)}, bf16[128,4096]{1,0:T(8,128)(2,1)S(1)}, u32[]{:S(2)}, u32[]{:S(2)}) collective-permute-start(bf16[128,4096]{1,0:T(8,128)(2,1)S(1)} %constant_dynamic-update-slice_fusion.refs_0_), channel_id=1, source_target_pairs={{2,4},{3,5},{4,2},{5,3},{10,12},{11,13},{12,10},{13,11},{18,20},{1... | collective-permute-start | bytes 3145736 | tf_op jit(solution)/shard_map/ppermute | solution.py:131
  28.0 30.3 %collective-permute-start.3 = (bf16[128,4096]{1,0:T(8,128)(2,1)S(1)}, bf16[128,4096]{1,0:T(8,128)(2,1)S(1)}, u32[]{:S(2)}, u32[]{:S(2)}) collective-permute-start(bf16[128,4096]{1,0:T(8,128)(2,1)S(1)} %constant_dynamic-update-slice_fusion.refs_0_), channel_id=1, source_target_pairs={{0,2},{1,3},{2,0},{3,1},{4,6},{5,7},{6,4},{7,5},{8,10},{9,11},{10,... | collective-permute-start | bytes 3145736 | tf_op jit(solution)/shard_map/ppermute | solution.py:131
  35.1 25.3 %collective-permute-start.13 = (bf16[256,2048]{1,0:T(8,128)(2,1)S(1)}, bf16[256,2048]{1,0:T(8,128)(2,1)S(1)}, u32[]{:S(2)}, u32[]{:S(2)}) collective-permute-start(bf16[256,2048]{1,0:T(8,128)(2,1)S(1)} %pad_maximum_fusion.1), channel_id=1, source_target_pairs={{0,24},{1,25},{2,26},{3,27},{4,28},{5,29},{6,30},{7,31},{8,16},{9,... | collective-permute-start | bytes 3145736 | tf_op jit(solution)/shard_map/ppermute | solution.py:131
  37.3 46.3 %collective-permute-start.12 = (bf16[256,2048]{1,0:T(8,128)(2,1)S(1)}, bf16[256,2048]{1,0:T(8,128)(2,1)S(1)}, u32[]{:S(2)}, u32[]{:S(2)}) collective-permute-start(bf16[256,2048]{1,0:T(8,128)(2,1)S(1)} %pad_maximum_fusion.1), channel_id=1, source_target_pairs={{0,16},{1,17},{2,18},{3,19},{4,20},{5,21},{6,22},{7,23},{8,24},{9,... | collective-permute-start | bytes 3145736 | tf_op jit(solution)/shard_map/ppermute | solution.py:131
  37.6 46.6 %collective-permute-start.11 = (bf16[256,2048]{1,0:T(8,128)(2,1)S(1)}, bf16[256,2048]{1,0:T(8,128)(2,1)S(1)}, u32[]{:S(2)}, u32[]{:S(2)}) collective-permute-start(bf16[256,2048]{1,0:T(8,128)(2,1)S(1)} %pad_maximum_fusion.1), channel_id=1, source_target_pairs={{0,8},{1,9},{2,10},{3,11},{4,12},{5,13},{6,14},{7,15},{8,0},{9,1},... | collective-permute-start | bytes 3145736 | tf_op jit(solution)/shard_map/ppermute | solution.py:131
  58.3 37.0 %collective-permute-start.6 = (bf16[128,4096]{1,0:T(8,128)(2,1)S(1)}, bf16[128,4096]{1,0:T(8,128)(2,1)S(1)}, u32[]{:S(2)}, u32[]{:S(2)}) collective-permute-start(bf16[128,4096]{1,0:T(8,128)(2,1)S(1)} %collective-permute-done.4.refs_4_), channel_id=1, source_target_pairs={{2,0},{3,1},{4,6},{5,7},{10,8},{11,9},{12,14},{13,15},{18,16},{19,... | collective-permute-start | bytes 3145736 | tf_op jit(solution)/shard_map/ppermute | solution.py:131
  59.6 35.7 %collective-permute-start.5 = (bf16[128,4096]{1,0:T(8,128)(2,1)S(1)}, bf16[128,4096]{1,0:T(8,128)(2,1)S(1)}, u32[]{:S(2)}, u32[]{:S(2)}) collective-permute-start(bf16[128,4096]{1,0:T(8,128)(2,1)S(1)} %collective-permute-done.3.refs_1_), channel_id=1, source_target_pairs={{2,4},{3,5},{4,2},{5,3},{10,12},{11,13},{12,10},{13,11},{18,20},{1... | collective-permute-start | bytes 3145736 | tf_op jit(solution)/shard_map/ppermute | solution.py:131
  60.4 24.5 %collective-permute-start.14 = (bf16[128,2048]{1,0:T(8,128)(2,1)S(1)}, bf16[128,2048]{1,0:T(8,128)(2,1)S(1)}, u32[]{:S(2)}, u32[]{:S(2)}) collective-permute-start(bf16[128,2048]{1,0:T(8,128)(2,1)S(1)} %slice.8), channel_id=1, source_target_pairs={{0,6},{1,7},{6,0},{7,1},{8,14},{9,15},{14,8},{15,9},{16,22},{17,23... | collective-permute-start | bytes 1572872 | tf_op jit(solution)/shard_map/ppermute | solution.py:131
  83.6 13.4 %collective-permute-start.16 = (bf16[128,4096]{1,0:T(8,128)(2,1)S(1)}, bf16[128,4096]{1,0:T(8,128)(2,1)S(1)}, u32[]{:S(2)}, u32[]{:S(2)}) collective-permute-start(bf16[128,4096]{1,0:T(8,128)(2,1)S(1)} %constant_dynamic-update-slice_fusion.refs_0_), channel_id=1, source_target_pairs={{0,1},{1,0},{2,3},{3,2},{4,5},{5,4},{6,7},{7,6},{8,9},{9,8},{10,11... | collective-permute-start | bytes 3145736 | tf_op jit(solution)/shard_map/ppermute | solution.py:131
  84.1 13.4 %collective-permute-start.20 = (bf16[128,4096]{1,0:T(8,128)(2,1)S(1)}, bf16[128,4096]{1,0:T(8,128)(2,1)S(1)}, u32[]{:S(2)}, u32[]{:S(2)}) collective-permute-start(bf16[128,4096]{1,0:T(8,128)(2,1)S(1)} %collective-permute-done.4.refs_4_), channel_id=1, source_target_pairs={{0,1},{1,0},{2,3},{3,2},{4,5},{5,4},{6,7},{7,6},{8,9},{9,8},{10,11... | collective-permute-start | bytes 3145736 | tf_op jit(solution)/shard_map/ppermute | solution.py:131
  84.9 14.0 %collective-permute-start.17 = (bf16[128,4096]{1,0:T(8,128)(2,1)S(1)}, bf16[128,4096]{1,0:T(8,128)(2,1)S(1)}, u32[]{:S(2)}, u32[]{:S(2)}) collective-permute-start(bf16[128,4096]{1,0:T(8,128)(2,1)S(1)} %collective-permute-done.3.refs_1_), channel_id=1, source_target_pairs={{0,1},{1,0},{2,3},{3,2},{4,5},{5,4},{6,7},{7,6},{8,9},{9,8},{10,11... | collective-permute-start | bytes 3145736 | tf_op jit(solution)/shard_map/ppermute | solution.py:131
  95.3 6.2 %collective-permute-start.19 = (bf16[128,4096]{1,0:T(8,128)(2,1)S(1)}, bf16[128,4096]{1,0:T(8,128)(2,1)S(1)}, u32[]{:S(2)}, u32[]{:S(2)}) collective-permute-start(bf16[128,4096]{1,0:T(8,128)(2,1)S(1)} %collective-permute-done.6.refs_3_), channel_id=1, source_target_pairs={{0,1},{1,0},{2,3},{3,2},{4,5},{5,4},{6,7},{7,6},{8,9},{9,8},{10,11... | collective-permute-start | bytes 3145736 | tf_op jit(solution)/shard_map/ppermute | solution.py:131
  97.0 4.5 %collective-permute-start.18 = (bf16[128,4096]{1,0:T(8,128)(2,1)S(1)}, bf16[128,4096]{1,0:T(8,128)(2,1)S(1)}, u32[]{:S(2)}, u32[]{:S(2)}) collective-permute-start(bf16[128,4096]{1,0:T(8,128)(2,1)S(1)} %collective-permute-done.5.refs_2_), channel_id=1, source_target_pairs={{0,1},{1,0},{2,3},{3,2},{4,5},{5,4},{6,7},{7,6},{8,9},{9,8},{10,11... | collective-permute-start | bytes 3145736 | tf_op jit(solution)/shard_map/ppermute | solution.py:131
  97.0 4.5 %collective-permute-start.21 = (bf16[128,2048]{1,0:T(8,128)(2,1)S(1)}, bf16[128,2048]{1,0:T(8,128)(2,1)S(1)}, u32[]{:S(2)}, u32[]{:S(2)}) collective-permute-start(bf16[128,2048]{1,0:T(8,128)(2,1)S(1)} %collective-permute-done.14.refs_5_), channel_id=1, source_target_pairs={{0,1},{1,0},{2,3},{3,2},{4,5},{5,4},{6,7},{7,6},{8,9},{9,8},{10,11... | collective-permute-start | bytes 1572872 | tf_op jit(solution)/shard_map/ppermute | solution.py:131
  97.6 17.0 %collective-permute-start.15 = (bf16[128,2048]{1,0:T(8,128)(2,1)S(1)}, bf16[128,2048]{1,0:T(8,128)(2,1)S(1)}, u32[]{:S(2)}, u32[]{:S(2)}) collective-permute-start(bf16[128,2048]{1,0:T(8,128)(2,1)S(1)} %slice.7), channel_id=1, source_target_pairs={{2,0},{3,1},{4,6},{5,7},{10,8},{11,9},{12,14},{13,15},{18,16},{19,... | collective-permute-start | bytes 1572872 | tf_op jit(solution)/shard_map/ppermute | solution.py:131
  114.6 2.8 %collective-permute-start.22 = (bf16[128,2048]{1,0:T(8,128)(2,1)S(1)}, bf16[128,2048]{1,0:T(8,128)(2,1)S(1)}, u32[]{:S(2)}, u32[]{:S(2)}) collective-permute-start(bf16[128,2048]{1,0:T(8,128)(2,1)S(1)} %collective-permute-done.15.refs_5_), channel_id=1, source_target_pairs={{0,1},{1,0},{2,3},{3,2},{4,5},{5,4},{6,7},{7,6},{8,9},{9,8},{10,11... | collective-permute-start | bytes 1572872 | tf_op jit(solution)/shard_map/ppermute | solution.py:131
